TPU v7x, 128 devices: a whole 4x4x4 slice. The times are simulated.
128 devices in a mesh: seq: 16 (over x, z), tp: 8 (over y, core).
Axes of the slice: x: 4, y: 4, z: 4, core: 2. Of those that a mesh axis runs over, the one named last changes fastest.
Arguments:
- queries: bfloat16 [4096, 8192], P('seq', 'tp'), may hold values from -1000 to 1000
- states: bfloat16 [8192, 4096], P('seq', 'tp'), may hold values from -18 to 18
- state_doc: int32 [8192], replicated, may hold values from 0 to 15, as said below
- state_pos: int32 [8192], replicated, may hold values from 0 to 511, as said below
- lengths: int32 [16], replicated, may hold values from 64 to 512, as said below
- offsets: int32 [16], replicated, may hold values from 0 to 256
- key_weight: bfloat16 [4096, 8192], P(None, 'tp'), may hold values from -1 to 1
- value_weight: bfloat16 [4096, 8192], P(None, 'tp'), may hold values from -1 to 1
- context_grad: bfloat16 [4096, 8192], P('seq', 'tp'), may hold values from -6 to 6
Outputs:
- query_grad: bfloat16 [4096, 8192], P('seq', 'tp')
- key_weight_grad: bfloat16 [4096, 8192], P('seq', 'tp')
- value_weight_grad: bfloat16 [4096, 8192], P('seq', 'tp')
Inputs may be any that keep to these rules, and one draw needn't show every extreme that they name: `state_doc`: each document has exactly 512 state rows. The 512 rows held by one index of seq name any one document at most 56 times, and in every draw some device's rows name some document exactly 56 times. `state_pos`: within one document the state rows carry each position from 0 to 511 exactly once. `lengths`: some document has length 512.
All inputs are finite; a program needn't handle non-finite values.
Results may differ from a plain program's by a relative error of at most 0.017.
Values may be sent and summed in bfloat16 or wider, within the bound.
A program may use at most 128 MiB of HBM per device.

v0:
```python
import jax
import jax.numpy as jnp
from jax import lax
from jax.sharding import PartitionSpec as P

HEAD_DIM = 128


def attend(query_rows, key_rows, value_rows, grad_rows, length, offset):
    query_count = query_rows.shape[0]
    state_count = key_rows.shape[0]
    head_count = query_rows.shape[1] // HEAD_DIM
    query_heads = query_rows.reshape(query_count, head_count, HEAD_DIM)
    key_heads = key_rows.reshape(state_count, head_count, HEAD_DIM)
    value_heads = value_rows.reshape(state_count, head_count, HEAD_DIM)
    grad_heads = grad_rows.reshape(query_count, head_count, HEAD_DIM)
    score_scale = HEAD_DIM ** (-0.5)
    scores = (
        jnp.einsum("qhd,khd->hqk", query_heads, key_heads, preferred_element_type=jnp.float32)
        * score_scale
    )
    query_index = jnp.arange(query_count)
    positions = jnp.arange(state_count)
    visible = (positions[None, :] <= offset + query_index[:, None]) & (positions[None, :] < length)
    scores = jnp.where(visible[None], scores, -jnp.inf)
    row_top = jnp.max(scores, axis=-1, keepdims=True)
    weights = jnp.exp(scores - row_top)
    probabilities = weights / jnp.sum(weights, axis=-1, keepdims=True)
    probs_low = probabilities.astype(jnp.bfloat16)
    context = jnp.einsum("hqk,khd->qhd", probs_low, value_heads, preferred_element_type=jnp.float32)
    delta_rows = jnp.sum(grad_heads.astype(jnp.float32) * context, axis=-1)
    prob_grad = jnp.einsum(
        "qhd,khd->hqk", grad_heads, value_heads, preferred_element_type=jnp.float32
    )
    score_grad = (probabilities * (prob_grad - delta_rows.T[:, :, None]) * score_scale).astype(
        jnp.bfloat16
    )
    query_grad = jnp.einsum(
        "hqk,khd->qhd", score_grad, key_heads, preferred_element_type=jnp.float32
    )
    key_grad = jnp.einsum(
        "hqk,qhd->khd", score_grad, query_heads, preferred_element_type=jnp.float32
    )
    value_grad = jnp.einsum(
        "hqk,qhd->khd", probs_low, grad_heads, preferred_element_type=jnp.float32
    )
    width = query_rows.shape[1]
    return (
        query_grad.astype(jnp.bfloat16).reshape(query_count, width),
        key_grad.astype(jnp.bfloat16).reshape(state_count, width),
        value_grad.astype(jnp.bfloat16).reshape(state_count, width),
    )


def shards(
    queries, states, state_doc, state_pos, lengths, offsets, key_weight, value_weight, context_grad
):
    seq_count = lax.axis_size("seq")
    device = lax.axis_index("seq")
    row_count = states.shape[0]
    capacity = 3 * row_count // (4 * seq_count) + row_count // 16
    docs_all = state_doc.reshape(seq_count, row_count)
    positions_all = state_pos.reshape(seq_count, row_count)
    onehot = (docs_all[:, :, None] == jnp.arange(seq_count)[None, None, :]).astype(jnp.int32)
    earlier = jnp.cumsum(onehot, axis=1) - onehot
    slots_all = jnp.sum(earlier * onehot, axis=2)
    own_docs = lax.dynamic_index_in_dim(docs_all, device, 0, keepdims=False)
    own_slots = lax.dynamic_index_in_dim(slots_all, device, 0, keepdims=False)
    targets = own_docs * capacity + own_slots
    source_row = jnp.full((seq_count * capacity,), row_count, jnp.int32)
    source_row = source_row.at[targets].set(jnp.arange(row_count, dtype=jnp.int32))
    arrival_index = jnp.arange(seq_count, dtype=jnp.int32)[:, None] * capacity + slots_all
    placed = jnp.where(docs_all == device, positions_all, row_count)
    order_slot = jnp.zeros((row_count,), jnp.int32)
    order_slot = order_slot.at[placed.reshape(-1)].set(arrival_index.reshape(-1), mode="drop")
    padded = jnp.concatenate([states, jnp.zeros((1, states.shape[1]), states.dtype)], axis=0)
    arrived = lax.all_to_all(
        jnp.take(padded, source_row, axis=0), "seq", split_axis=0, concat_axis=0, tiled=True
    )
    doc_states = lax.all_gather(jnp.take(arrived, order_slot, axis=0), "tp", axis=1, tiled=True)
    key_rows = jnp.dot(doc_states, key_weight, preferred_element_type=jnp.float32).astype(
        jnp.bfloat16
    )
    value_rows = jnp.dot(doc_states, value_weight, preferred_element_type=jnp.float32).astype(
        jnp.bfloat16
    )
    length = lax.dynamic_index_in_dim(lengths, device, 0, keepdims=False)
    offset = lax.dynamic_index_in_dim(offsets, device, 0, keepdims=False)
    query_grad, key_grad, value_grad = attend(
        queries, key_rows, value_rows, context_grad, length, offset
    )
    both_grads = jnp.concatenate([key_grad, value_grad], axis=1)
    summed = lax.psum_scatter(
        lax.dot_general(
            doc_states, both_grads, (((0,), (0,)), ((), ())), preferred_element_type=jnp.float32
        ).astype(jnp.bfloat16),
        "seq",
        scatter_dimension=0,
        tiled=True,
    ).astype(jnp.float32)
    head_width = key_weight.shape[1]
    return (
        query_grad,
        summed[:, :head_width].astype(jnp.bfloat16),
        summed[:, head_width:].astype(jnp.bfloat16),
    )


def solution(mesh):
    in_specs = (
        P("seq", "tp"),
        P("seq", "tp"),
        P(),
        P(),
        P(),
        P(),
        P(None, "tp"),
        P(None, "tp"),
        P("seq", "tp"),
    )
    out_specs = (P("seq", "tp"), P("seq", "tp"), P("seq", "tp"))
    return jax.shard_map(shards, mesh=mesh, in_specs=in_specs, out_specs=out_specs, check_vma=False)
```

profile of v0, /device:TPU:1, one launch (start us, length us, event | category | flops | bytes accessed | tf_op | source)
XLA Modules:
  0.0 280.3 jit_solution(13392253341646939702)
XLA Ops:
  7.2 0.8 eq.34
  8.0 0.8 fusion.16
  8.8 18.1 %reduce-window.6 = s32[16,16,4,128]{3,1,2,0:T(8,128)S(1)} reduce-window(s32[16,16,4,128]{3,1,2,0:T(8,128)S(1)} %fusion.16, s32[]{:T(128)} %constant.34.clone.1), window={size=1x1x1x128 pad=0_0x0_0x0_0x127_0}, to_apply=%region_0.0 | reduce-window | flops 16646144 | bytes 1048580 | tf_op jit(solution)/shard_map/reduce-window
  28.1 2.4 scatter_custom_fusion.1
  30.7 3.5 %gather_fusion = bf16[896,512]{1,0:T(8,128)(2,1)S(1)} fusion(bf16[513,512]{1,0:T(8,128)(2,1)S(1)} %concatenate.6, s32[1024]{0:T(1024)S(1)} %pad_clamp_fusion.1), kind=kCustom, calls=%fused_computation | custom fusion | bytes 1838592 | tf_op jit(solution)/shard_map/jit(_take)/gather | solution.py:78
  34.2 1.1 broadcast_select_fusion
  35.4 8.5 %all-to-all-start = ((bf16[16,56,512]{2,1,0:T(8,128)(2,1)}), bf16[16,56,512]{2,1,0:T(8,128)(2,1)S(1)}, u32[]{:S(2)}, u32[]{:S(2)}) async-start(bf16[16,56,512]{2,1,0:T(8,128)(2,1)} %broadcast_select_fusion), calls=%async_computation | async-start | bytes 1835008 | tf_op jit(solution)/shard_map/all_to_all | solution.py:77
  44.1 30.4 %scatter_custom_fusion = s32[512]{0:T(512)S(1)} fusion(s32[8192]{0:T(1024)S(1)} %compare_select_fusion, s32[8192]{0:T(1024)S(1)} %bitcast.106, s32[]{:T(128)} %constant.34.clone.1), kind=kCustom, calls=%fused_computation.56 | custom fusion | bytes 2052 | tf_op jit(solution)/shard_map/scatter | solution.py:75
  74.6 2.0 gather_fusion.1
  76.6 0.9 broadcast_select_fusion.1
  77.8 0.6 dynamic_slice.16
  78.4 0.6 dynamic_slice.17
  79.4 0.7 iota_compare_fusion.3
  80.0 0.7 iota_add_fusion
  80.8 31.3 %all-gather.2.cloned.1.call-done = bf16[512,4096]{1,0:T(8,128)(2,1)} async-done(((bf16[512,512]{1,0:T(8,128)(2,1)}), bf16[512,4096]{1,0:T(8,128)(2,1)}) %all-gather.2.cloned.1.call-update) | async-done | bytes 4194320 | tf_op jit(solution)/shard_map/all_gather | solution.py:80
  112.2 9.1 %convolution_convert_fusion.1 = bf16[512,1024]{1,0:T(8,128)(2,1)S(1)} fusion(bf16[512,4096]{1,0:T(8,128)(2,1)} %all-gather.2.cloned.1.call-done, bf16[4096,1024]{1,0:T(8,128)(2,1)} %param.16), kind=kOutput, calls=%fused_computation.20 | convolution fusion | flops 4295491584 | bytes 13631488 | tf_op jit(solution)/shard_map/dot_general | solution.py:84
  121.3 0.5 copy.48
  121.9 10.5 %convolution_convert_fusion.2 = bf16[512,1024]{1,0:T(8,128)(2,1)} fusion(bf16[512,4096]{1,0:T(8,128)(2,1)} %all-gather.2.cloned.1.call-done, bf16[4096,1024]{1,0:T(8,128)(2,1)} %param.15), kind=kOutput, calls=%fused_computation.21 | convolution fusion | flops 4295491584 | bytes 13631488 | tf_op jit(solution)/shard_map/dot_general | solution.py:81
  132.4 1.5 copy.46
  133.9 3.4 %fusion.30 = (f32[8,256]{1,0:T(8,128)S(1)}, f32[8,256,512]{1,2,0:T(8,128)}) fusion(pred[256,512]{0,1:T(8,128)(4,1)S(1)} %fusion.17, bf16[512,8,128]{0,2,1:T(8,128)(2,1)S(1)} %bitcast.95, bf16[256,8,128]{0,2,1:T(8,128)(2,1)S(1)} %bitcast.100), kind=kOutput, calls=%fused_computation.63 | convolution fusion | flops 272630272 | bytes 5906432 | tf_op jit(solution)/shard_map/sub | solution.py:27
  137.3 2.5 fusion.10
  139.9 0.8 convolution_convert_fusion.3
  140.7 0.5 fusion.12
  141.2 0.8 copy-done.3
  142.1 2.2 fusion.2
  144.3 0.8 convolution_convert_fusion.4
  145.1 15.8 %convolution_convert_fusion = bf16[4096,2048]{1,0:T(8,128)(2,1)} fusion(bf16[512,4096]{1,0:T(8,128)(2,1)} %all-gather.2.cloned.1.call-done, bf16[512,1024]{0,1:T(8,128)(2,1)S(1)} %bitcast.103, bf16[512,1024]{0,1:T(8,128)(2,1)S(1)} %bitcast.104), kind=kOutput, calls=%fused_computation.5 | convolution fusion | flops 8602517504 | bytes 23068672 | tf_op jit(solution)/shard_map/dot_general | solution.py:94
  161.0 1.2 copy-done.1
  162.2 1.3 convolution_convert_fusion.5
  163.4 2.0 copy.40
  165.5 105.7 %reduce-scatter.2.cloned.1.call-done = bf16[256,2048]{1,0:T(8,128)(2,1)} async-done(((bf16[4096,2048]{1,0:T(8,128)(2,1)}), bf16[256,2048]{1,0:T(8,128)(2,1)}) %reduce-scatter.2.cloned.1.call-update) | async-done | bytes 1048592 | tf_op jit(solution)/shard_map/reduce_scatter | solution.py:93
  271.2 2.2 fusion.29
  (48 shorter events, 2.2 us)
Async XLA Ops:
  7.2 23.5 %copy-start.6 = (bf16[512,512]{1,0:T(8,128)(2,1)S(1)}, bf16[512,512]{1,0:T(8,128)(2,1)}, u32[]{:S(2)}) copy-start(bf16[512,512]{1,0:T(8,128)(2,1)} %param.10) | copy-start | bytes 1572868
  30.7 13.4 %copy-start.7 = (s32[8192]{0:T(1024)S(1)}, s32[8192]{0:T(1024)}, u32[]{:S(2)}) copy-start(s32[8192]{0:T(1024)} %param.11) | copy-start | bytes 98308
  30.7 13.4 %copy-start.8 = (s32[8192]{0:T(1024)S(1)}, s32[8192]{0:T(1024)}, u32[]{:S(2)}) copy-start(s32[8192]{0:T(1024)} %param.12) | copy-start | bytes 98308
  35.4 42.4 %copy-start.9 = (s32[16]{0:T(128)S(1)}, s32[16]{0:T(128)}, u32[]{:S(2)}) copy-start(s32[16]{0:T(128)} %param.14) | copy-start | bytes 196
  35.4 43.0 %copy-start.10 = (s32[16]{0:T(128)S(1)}, s32[16]{0:T(128)}, u32[]{:S(2)}) copy-start(s32[16]{0:T(128)} %param.13) | copy-start | bytes 196
  35.4 43.6 %copy-start.4 = (bf16[256,1024]{1,0:T(8,128)(2,1)S(1)}, bf16[256,1024]{1,0:T(8,128)(2,1)}, u32[]{:S(2)}) copy-start(bf16[256,1024]{1,0:T(8,128)(2,1)} %param.9) | copy-start | bytes 1572868
  35.4 39.2 %all-to-all-start = ((bf16[16,56,512]{2,1,0:T(8,128)(2,1)}), bf16[16,56,512]{2,1,0:T(8,128)(2,1)S(1)}, u32[]{:S(2)}, u32[]{:S(2)}) async-start(bf16[16,56,512]{2,1,0:T(8,128)(2,1)} %broadcast_select_fusion), calls=%async_computation | async-start | bytes 1835008 | tf_op jit(solution)/shard_map/all_to_all | solution.py:77
  43.9 35.2 %copy-start.5 = (bf16[256,1024]{1,0:T(8,128)(2,1)S(1)}, bf16[256,1024]{1,0:T(8,128)(2,1)}, u32[]{:S(2)}) copy-start(bf16[256,1024]{1,0:T(8,128)(2,1)} %param.17) | copy-start | bytes 1572868
  43.9 68.2 %all-gather.2.cloned.1.call-start = ((), (), s32[]{:S(2)}) async-start(), calls=%async_computation.2 | async-start | bytes 4718592 | tf_op jit(solution)/shard_map/all_gather | solution.py:80
  77.5 193.7 %reduce-scatter.2.cloned.1.call-start = ((), (), s32[]{:S(2)}) async-start(), calls=%async_computation.3 | async-start | bytes 17825792 | tf_op jit(solution)/shard_map/reduce_scatter | solution.py:93
  121.9 18.8 %copy-start.2 = (bf16[512,1024]{0,1:T(8,128)(2,1)}, bf16[512,1024]{0,1:T(8,128)(2,1)S(1)}, u32[]{:S(2)}) copy-start(bf16[512,1024]{0,1:T(8,128)(2,1)S(1)} %copy.48) | copy-start | bytes 3145732
  133.9 3.5 %copy-start = (bf16[512,1024]{0,1:T(8,128)(2,1)}, bf16[512,1024]{0,1:T(8,128)(2,1)S(1)}, u32[]{:S(2)}) copy-start(bf16[512,1024]{0,1:T(8,128)(2,1)S(1)} %copy.46) | copy-start | bytes 3145732
  139.9 2.2 copy-start.3
  160.9 1.2 copy-start.1
Sparse Core Ops, SparseCore 0:
  77.7 34.4 all-gather.1
  161.1 110.0 reduce-scatter.1
where the time goes:
time: 281 us; the launch traced here: 280 us
  waiting for transfers between devices  137 us (49%)
  local copies, waits for them, and re-layouts  50 us (18%)
  matrix products  44.5 us (16%)
  other arithmetic  25.5 us (9%)
  between operations  14.4 us (5%)
  starting transfers between devices  8.81 us (3%)
    reduce_scatter x1, waiting for transfers between devices, shards(): lax.psum_scatter(lax.dot_general(doc_states, both_grads, (((0,), (0,)), (...  106 us
    all_gather x1, waiting for transfers between devices, shards(): lax.all_gather(jnp.take(arrived, order_slot, axis=0), 'tp', axis=1, tiled...  31.3 us
    scatter x1, local copies, waits for them, and re-layouts, shards(): order_slot.at[placed.reshape(-1)]  30.4 us
    another operation x2, other arithmetic  18.3 us
    dot_general x1, matrix products, shards(): lax.dot_general(doc_states, both_grads, (((0,), (0,)), ((), ())), preferr...  15.8 us
    dot_general x1, matrix products, shards(): jnp.dot(doc_states, key_weight, preferred_element_type=jnp.float32)  10.5 us
    dot_general x1, matrix products, shards(): jnp.dot(doc_states, value_weight, preferred_element_type=jnp.float32)  9.14 us
    all_to_all x1, starting transfers between devices, shards(): lax.all_to_all(jnp.take(padded, source_row, axis=0), 'seq', split_axis=0,...  8.55 us
  transfers between devices with their start and end apart: 3, of which 2 were waited for; matrix products, arithmetic and copies ran while one was open for 13% of the time, Pallas kernels for 0%

commit v1 on v0

v1 whole, which is shorter than its diff:
```python
import functools

import jax
import jax.numpy as jnp
from jax import lax
from jax.experimental import pallas as pl
from jax.experimental.pallas import tpu as pltpu
from jax.sharding import PartitionSpec as P

HEAD_DIM = 128
SLOTS = 64
F32 = jnp.float32
BF16 = jnp.bfloat16


def dot_nt(a, b):
    return lax.dot_general(a, b, (((1,), (1,)), ((), ())), preferred_element_type=F32)


def dot_tn(a, b):
    return lax.dot_general(a, b, (((0,), (0,)), ((), ())), preferred_element_type=F32)


def strict_upper(n):
    return (lax.broadcasted_iota(jnp.int32, (n, n), 0) < lax.broadcasted_iota(jnp.int32, (n, n), 1)).astype(F32).astype(BF16)


def pack_table(doc_ref, me, docs, rows):
    own = jnp.concatenate([doc_ref[pl.ds(4 * me + j, 1), :] for j in range(4)], axis=1)
    member = lax.broadcasted_iota(jnp.int32, (docs, rows), 0) == own
    member_f = member.astype(F32)
    ranks = jnp.dot(member_f.astype(BF16), strict_upper(rows), preferred_element_type=F32)
    rank = jnp.sum(ranks * member_f, axis=0, keepdims=True).astype(jnp.int32)
    target = own * SLOTS + rank
    hot = lax.broadcasted_iota(jnp.int32, (docs * SLOTS, rows), 0) == target
    return hot.astype(F32).astype(BF16)


def order_table(doc_ref, pos_ref, me, docs, rows):
    docs_all = jnp.concatenate([doc_ref[pl.ds(j, docs, stride=4), :] for j in range(4)], axis=1)
    pos_all = jnp.concatenate([pos_ref[pl.ds(j, docs, stride=4), :] for j in range(4)], axis=1)
    member = docs_all == me
    member_f = member.astype(F32)
    ranks = jnp.dot(member_f.astype(BF16), strict_upper(rows), preferred_element_type=F32).astype(jnp.int32)
    ranks = jnp.where(member, ranks, -1)
    high = (pos_all // 2).astype(F32)
    low = (pos_all % 2).astype(F32)
    parts = []
    for s in range(docs):
        hot = (lax.broadcasted_iota(jnp.int32, (SLOTS, rows), 0) == ranks[s:s + 1, :]).astype(F32).astype(BF16)
        three = jnp.concatenate([high[s:s + 1], low[s:s + 1], jnp.ones((1, rows), F32), jnp.zeros((5, rows), F32)], axis=0)
        parts.append(dot_nt(three.astype(BF16), hot))
    table = jnp.concatenate(parts, axis=1)
    slot_pos = (2.0 * table[0:1] + table[1:2] + table[2:3]).astype(jnp.int32) - 1
    hot = lax.broadcasted_iota(jnp.int32, (rows, docs * SLOTS), 0) == slot_pos
    return hot.astype(F32).astype(BF16)


def tables_kernel(docs, rows, doc_ref, pos_ref, pack_ref, order_ref):
    me = lax.axis_index("seq")
    pack_ref[...] = pack_table(doc_ref, me, docs, rows)
    order_ref[...] = order_table(doc_ref, pos_ref, me, docs, rows)


def attention_head(q, k, v, g, length, offset):
    scale = HEAD_DIM ** (-0.5)
    queries, rows = q.shape[0], k.shape[0]
    scores = dot_nt(q, k) * scale
    index = lax.broadcasted_iota(jnp.int32, (queries, rows), 0)
    pos = lax.broadcasted_iota(jnp.int32, (queries, rows), 1)
    visible = (pos <= index + offset) & (pos < length)
    scores = jnp.where(visible, scores, -jnp.inf)
    weights = jnp.exp(scores - jnp.max(scores, axis=1, keepdims=True))
    probs = weights * (1.0 / jnp.sum(weights, axis=1, keepdims=True))
    low = probs.astype(BF16)
    prob_grad = dot_nt(g, v)
    delta = jnp.sum(low.astype(F32) * prob_grad, axis=1, keepdims=True)
    score_grad = (probs * (prob_grad - delta) * scale).astype(BF16)
    q_grad = jnp.dot(score_grad, k, preferred_element_type=F32).astype(BF16)
    k_grad = dot_tn(q, score_grad).astype(BF16)
    v_grad = dot_tn(g, low).astype(BF16)
    return q_grad, k_grad, v_grad


def attention_kernel(len_ref, off_ref, q_ref, k_ref, v_ref, g_ref, qg_ref, kg_ref, vg_ref):
    me = lax.axis_index("seq")
    qg, kg, vg = attention_head(q_ref[...], k_ref[...], v_ref[...], g_ref[...], len_ref[me], off_ref[me])
    qg_ref[...] = qg
    kg_ref[...] = kg
    vg_ref[...] = vg


def attention(queries, keys, values, grads, lengths, offsets):
    count, width = queries.shape
    rows = keys.shape[0]
    col = lambda n: pl.BlockSpec((n, HEAD_DIM), lambda h, *_: (0, h))
    row = lambda n: pl.BlockSpec((HEAD_DIM, n), lambda h, *_: (h, 0))
    return pl.pallas_call(
        attention_kernel,
        grid_spec=pltpu.PrefetchScalarGridSpec(
            num_scalar_prefetch=2, grid=(width // HEAD_DIM,),
            in_specs=[col(count), col(rows), col(rows), col(count)],
            out_specs=[col(count), row(rows), row(rows)]),
        out_shape=[jax.ShapeDtypeStruct((count, width), BF16), jax.ShapeDtypeStruct((width, rows), BF16),
                   jax.ShapeDtypeStruct((width, rows), BF16)],
        cost_estimate=pl.CostEstimate(flops=12 * count * rows * width, bytes_accessed=8 * rows * width, transcendentals=0),
        name="attention",
    )(lengths, offsets, queries, keys, values, grads)


def shards(queries, states, state_doc, state_pos, lengths, offsets, key_weight, value_weight, context_grad):
    docs = lax.axis_size("seq")
    rows = states.shape[0]
    pack, order = pl.pallas_call(
        functools.partial(tables_kernel, docs, rows),
        out_shape=[jax.ShapeDtypeStruct((docs * SLOTS, rows), BF16), jax.ShapeDtypeStruct((rows, docs * SLOTS), BF16)],
        in_specs=[pl.BlockSpec(memory_space=pltpu.VMEM)] * 2,
        out_specs=[pl.BlockSpec(memory_space=pltpu.VMEM)] * 2,
        name="tables",
    )(state_doc.reshape(-1, 128), state_pos.reshape(-1, 128))
    packed = jnp.dot(pack, states, preferred_element_type=F32).astype(BF16)
    arrived = lax.all_to_all(packed, "seq", split_axis=0, concat_axis=0, tiled=True)
    own = jnp.dot(order, arrived, preferred_element_type=F32).astype(BF16)
    doc_states = lax.all_gather(own, "tp", axis=1, tiled=True)
    key_rows = jnp.dot(doc_states, key_weight, preferred_element_type=F32).astype(BF16)
    value_rows = jnp.dot(doc_states, value_weight, preferred_element_type=F32).astype(BF16)
    query_grad, key_grad, value_grad = attention(queries, key_rows, value_rows, context_grad, lengths, offsets)
    both = jnp.concatenate([key_grad, value_grad], axis=0)
    parts = lax.dot_general(doc_states, both, (((0,), (1,)), ((), ())), preferred_element_type=F32).astype(BF16)
    summed = lax.psum_scatter(parts, "seq", scatter_dimension=0, tiled=True)
    width = key_weight.shape[1]
    return query_grad, summed[:, :width], summed[:, width:]


def solution(mesh):
    in_specs = (P("seq", "tp"), P("seq", "tp"), P(), P(), P(), P(), P(None, "tp"), P(None, "tp"), P("seq", "tp"))
    out_specs = (P("seq", "tp"), P("seq", "tp"), P("seq", "tp"))
    return jax.shard_map(shards, mesh=mesh, in_specs=in_specs, out_specs=out_specs, check_vma=False)
```

time: 281 us -> 233 us (0.83)
  local copies, waits for them, and re-layouts: 50 us -> 2.25 us
  other arithmetic: 25.5 us -> 0 us
  blocking collectives: 0 us -> 24.2 us
  Pallas kernels: 0 us -> 12.8 us
  starting transfers between devices: 8.81 us -> 0.26 us
  matrix products: 44.5 us -> 36.4 us
  waiting for transfers between devices: 137 us -> 142 us
    scatter x2 -> x0, local copies, waits for them, and re-layouts: 32.9 us -> none  [the longest x1 30.4 us: shards(): order_slot.at[placed.reshape(-1)]]
    all_to_all x0 -> x1, blocking collectives: none -> 24.2 us  [shards(): lax.all_to_all(packed, 'seq', split_axis=0, concat_axis=0, tiled=True)]
    another operation x2 -> x0, other arithmetic: 18.3 us -> none
    pallas_call x0 -> x2, Pallas kernels: none -> 12.8 us  [the longest x1 9.66 us: attention(): pl.pallas_call(attention_kernel, grid_spec=pltpu.PrefetchScalarGridSpec(n...]
    all_to_all x1 -> x0, starting transfers between devices: 8.55 us -> none  [shards(): lax.all_to_all(jnp.take(padded, source_row, axis=0), 'seq', split_axis=0,...]
    gather x2 -> x0, local copies, waits for them, and re-layouts: 5.48 us -> none  [the longest x1 3.51 us: shards(): jnp.take(padded, source_row, axis=0)]
    dot_general x8 -> x5, matrix products: 41.1 us -> 36.4 us  [the longest x1 14.6 us: shards(): lax.dot_general(doc_states, both, (((0,), (1,)), ((), ())), preferred_ele...]
    reduce_scatter x1, waiting for transfers between devices: 106 us -> 110 us  [shards(): summed = lax.psum_scatter(parts, 'seq', scatter_dimension=0, tiled=True)]
  transfers between devices with their start and end apart: 3 -> 2, of which waited for: 2 -> 2; matrix products, arithmetic and copies ran while one was open for 13% -> 0% of each run, Pallas kernels for 0% -> 0%
where the time goes in v1:
time: 233 us; the launch traced here: 232 us
  waiting for transfers between devices  142 us (61%)
  matrix products  36.4 us (16%)
  blocking collectives  24.2 us (10%)
  between operations  14.1 us (6%)
  Pallas kernels  12.8 us (5%)
    reduce_scatter x1, waiting for transfers between devices, shards(): summed = lax.psum_scatter(parts, 'seq', scatter_dimension=0, tiled=True)  110 us
    all_gather x1, waiting for transfers between devices, shards(): doc_states = lax.all_gather(own, 'tp', axis=1, tiled=True)  31.9 us
    all_to_all x1, blocking collectives, shards(): lax.all_to_all(packed, 'seq', split_axis=0, concat_axis=0, tiled=True)  24.2 us
    dot_general x1, matrix products, shards(): lax.dot_general(doc_states, both, (((0,), (1,)), ((), ())), preferred_ele...  14.6 us
    dot_general x1, matrix products, shards(): jnp.dot(doc_states, value_weight, preferred_element_type=F32).astype(BF16)  10.3 us
    pallas_call x1, Pallas kernels, attention(): pl.pallas_call(attention_kernel, grid_spec=pltpu.PrefetchScalarGridSpec(n...  9.66 us
    dot_general x1, matrix products, shards(): jnp.dot(doc_states, key_weight, preferred_element_type=F32).astype(BF16)  7.97 us
  transfers between devices with their start and end apart: 2, of which 2 were waited for; matrix products, arithmetic and copies ran while one was open for 0% of the time, Pallas kernels for 0%

profile of v1, /device:TPU:1, one launch (start us, length us, event | category | flops | bytes accessed | tf_op | source)
XLA Modules:
  0.0 232.2 jit_solution(6290895294947700798)
XLA Ops:
  7.2 0.0 copy-start
  7.2 0.0 all-gather.2.cloned.1.call-start
  7.2 3.2 %tables.1 = (bf16[1024,512]{1,0:T(8,128)(2,1)}, bf16[512,1024]{1,0:T(8,128)(2,1)}) custom-call(s32[64,128]{1,0:T(8,128)} %bitcast.15, s32[64,128]{1,0:T(8,128)} %bitcast.16), custom_call_target="tpu_custom_call" | custom-call | tf_op jit(solution)/shard_map/tables/pallas_call | solution.py:114
  10.4 0.0 copy-start.2
  10.4 0.0 copy-done
  10.4 2.0 convolution_convert_fusion.3
  12.4 24.2 %all_to_all.12 = bf16[16,64,512]{2,1,0:T(8,128)(2,1)S(1)} all-to-all(bf16[16,64,512]{2,1,0:T(8,128)(2,1)S(1)} %bitcast.14), channel_id=1, replica_groups=mesh['seq'=16,'tp'=8] {'seq'}, dimensions={0} | all-to-all | bytes 2097152 | tf_op jit(solution)/shard_map/all_to_all | solution.py:122
  36.6 0.0 copy-done.2
  36.6 1.5 convolution_convert_fusion.4
  38.1 0.0 all-gather.2.cloned.1.call-update
  38.1 0.2 reduce-scatter.2.cloned.1.call-start
  38.3 31.9 %all-gather.2.cloned.1.call-done = bf16[512,4096]{1,0:T(8,128)(2,1)} async-done(((bf16[512,512]{1,0:T(8,128)(2,1)}), bf16[512,4096]{1,0:T(8,128)(2,1)}) %all-gather.2.cloned.1.call-update) | async-done | bytes 4194320 | tf_op jit(solution)/shard_map/all_gather | solution.py:124
  70.3 0.0 copy-start.1
  70.3 10.3 %convolution_convert_fusion.1.v_ref = bf16[512,1024]{1,0:T(8,128)(2,1)} fusion(bf16[512,4096]{1,0:T(8,128)(2,1)} %all-gather.2.cloned.1.call-done, bf16[4096,1024]{1,0:T(8,128)(2,1)} %param.16), kind=kOutput, calls=%fused_computation.4 | convolution fusion | flops 4295491584 | bytes 13631488 | tf_op jit(solution)/shard_map/dot_general | solution.py:126
  80.6 0.0 copy-done.1
  80.6 8.0 %convolution_convert_fusion.2.k_ref = bf16[512,1024]{1,0:T(8,128)(2,1)} fusion(bf16[512,4096]{1,0:T(8,128)(2,1)S(1)} %copy-done.1, bf16[4096,1024]{1,0:T(8,128)(2,1)} %param.15), kind=kOutput, calls=%fused_computation.5 | convolution fusion | flops 4295491584 | bytes 13631488 | tf_op jit(solution)/shard_map/dot_general | solution.py:125
  88.5 9.7 %attention.1 = (bf16[256,1024]{1,0:T(8,128)(2,1)}, bf16[1024,512]{1,0:T(8,128)(2,1)}, bf16[1024,512]{1,0:T(8,128)(2,1)}) custom-call(s32[16]{0:T(128)} %len_ref.1, s32[16]{0:T(128)} %off_ref.1, bf16[256,1024]{1,0:T(8,128)(2,1)} %q_ref.1, bf16[512,1024]{1,0:T(8,128)(2,1)} %convolution_convert_fusion.2.k_ref, ...), custom_call_target="tpu_custom_call" | custom-call | flops 1610612736 | bytes 4194304 | tf_op jit(solution)/shard_map/attention/pallas_call | solution.py:98
  98.2 14.6 %convolution_convert_fusion = bf16[4096,2048]{1,0:T(8,128)(2,1)} fusion(bf16[512,4096]{1,0:T(8,128)(2,1)} %all-gather.2.cloned.1.call-done, bf16[1024,512]{1,0:T(8,128)(2,1)} %get-tuple-element.12, bf16[1024,512]{1,0:T(8,128)(2,1)} %get-tuple-element.11), kind=kOutput, calls=%fused_computation | convolution fusion | flops 8602517504 | bytes 23068672 | tf_op jit(solution)/shard_map/dot_general | solution.py:129
  112.8 0.0 reduce-scatter.2.cloned.1.call-update
  112.8 110.2 %reduce-scatter.2.cloned.1.call-done = bf16[256,2048]{1,0:T(8,128)(2,1)} async-done(((bf16[4096,2048]{1,0:T(8,128)(2,1)}), bf16[256,2048]{1,0:T(8,128)(2,1)}) %reduce-scatter.2.cloned.1.call-update) | async-done | bytes 1048592 | tf_op jit(solution)/shard_map/reduce_scatter | solution.py:130
  223.1 2.2 fusion.4
Async XLA Ops:
  7.2 3.2 %copy-start = (bf16[512,512]{1,0:T(8,128)(2,1)S(1)}, bf16[512,512]{1,0:T(8,128)(2,1)}, u32[]{:S(2)}) copy-start(bf16[512,512]{1,0:T(8,128)(2,1)} %param.10) | copy-start | bytes 1572868
  7.2 63.1 %all-gather.2.cloned.1.call-start = ((), (), s32[]{:S(2)}) async-start(), calls=%async_computation.2 | async-start | bytes 4718592 | tf_op jit(solution)/shard_map/all_gather | solution.py:124
  10.4 26.2 %copy-start.2 = (bf16[512,1024]{1,0:T(8,128)(2,1)S(1)}, bf16[512,1024]{1,0:T(8,128)(2,1)}, u32[]{:S(2)}) copy-start(bf16[512,1024]{1,0:T(8,128)(2,1)} %get-tuple-element.8) | copy-start | bytes 3145732
  38.1 185.0 %reduce-scatter.2.cloned.1.call-start = ((), (), s32[]{:S(2)}) async-start(), calls=%async_computation.3 | async-start | bytes 17825792 | tf_op jit(solution)/shard_map/reduce_scatter | solution.py:130
  70.3 10.3 %copy-start.1 = (bf16[512,4096]{1,0:T(8,128)(2,1)S(1)}, bf16[512,4096]{1,0:T(8,128)(2,1)}, u32[]{:S(2)}) copy-start(bf16[512,4096]{1,0:T(8,128)(2,1)} %all-gather.2.cloned.1.call-done) | copy-start | bytes 12582916
Sparse Core Ops, SparseCore 0:
  38.2 31.9 all-gather.1
  113.0 110.0 reduce-scatter.1

commit v2 on v1

v2 whole, which is shorter than its diff:
```python
import functools

import jax
import jax.numpy as jnp
from jax import lax
from jax.experimental import pallas as pl
from jax.experimental.pallas import tpu as pltpu
from jax.sharding import PartitionSpec as P

HEAD_DIM = 128
SLOTS = 64
F32 = jnp.float32
BF16 = jnp.bfloat16


def dot_nt(a, b):
    return lax.dot_general(a, b, (((1,), (1,)), ((), ())), preferred_element_type=F32)


def dot_tn(a, b):
    return lax.dot_general(a, b, (((0,), (0,)), ((), ())), preferred_element_type=F32)


def strict_upper(n):
    return (lax.broadcasted_iota(jnp.int32, (n, n), 0) < lax.broadcasted_iota(jnp.int32, (n, n), 1)).astype(F32).astype(BF16)


def pack_table(doc_ref, me, docs, rows):
    own = jnp.concatenate([doc_ref[pl.ds(4 * me + j, 1), :] for j in range(4)], axis=1)
    member = lax.broadcasted_iota(jnp.int32, (docs, rows), 0) == own
    member_f = member.astype(F32)
    ranks = jnp.dot(member_f.astype(BF16), strict_upper(rows), preferred_element_type=F32)
    rank = jnp.sum(ranks * member_f, axis=0, keepdims=True).astype(jnp.int32)
    target = own * SLOTS + rank
    hot = lax.broadcasted_iota(jnp.int32, (docs * SLOTS, rows), 0) == target
    return hot.astype(F32).astype(BF16)


def order_table(doc_ref, pos_ref, me, docs, rows):
    docs_all = jnp.concatenate([doc_ref[pl.ds(j, docs, stride=4), :] for j in range(4)], axis=1)
    pos_all = jnp.concatenate([pos_ref[pl.ds(j, docs, stride=4), :] for j in range(4)], axis=1)
    member = docs_all == me
    member_f = member.astype(F32)
    ranks = jnp.dot(member_f.astype(BF16), strict_upper(rows), preferred_element_type=F32).astype(jnp.int32)
    ranks = jnp.where(member, ranks, -1)
    high = (pos_all // 2).astype(F32)
    low = (pos_all % 2).astype(F32)
    parts = []
    for s in range(docs):
        hot = (lax.broadcasted_iota(jnp.int32, (SLOTS, rows), 0) == ranks[s:s + 1, :]).astype(F32).astype(BF16)
        three = jnp.concatenate([high[s:s + 1], low[s:s + 1], jnp.ones((1, rows), F32), jnp.zeros((5, rows), F32)], axis=0)
        parts.append(dot_nt(three.astype(BF16), hot))
    table = jnp.concatenate(parts, axis=1)
    slot_pos = (2.0 * table[0:1] + table[1:2] + table[2:3]).astype(jnp.int32) - 1
    hot = lax.broadcasted_iota(jnp.int32, (rows, docs * SLOTS), 0) == slot_pos
    return hot.astype(F32).astype(BF16)


def attention_head(q, k, v, g, length, offset):
    scale = HEAD_DIM ** (-0.5)
    queries, rows = q.shape[0], k.shape[0]
    scores = dot_nt(q, k) * scale
    index = lax.broadcasted_iota(jnp.int32, (queries, rows), 0)
    pos = lax.broadcasted_iota(jnp.int32, (queries, rows), 1)
    visible = (pos <= index + offset) & (pos < length)
    scores = jnp.where(visible, scores, -jnp.inf)
    weights = jnp.exp(scores - jnp.max(scores, axis=1, keepdims=True))
    probs = weights * (1.0 / jnp.sum(weights, axis=1, keepdims=True))
    low = probs.astype(BF16)
    prob_grad = dot_nt(g, v)
    delta = jnp.sum(low.astype(F32) * prob_grad, axis=1, keepdims=True)
    score_grad = (probs * (prob_grad - delta) * scale).astype(BF16)
    q_grad = jnp.dot(score_grad, k, preferred_element_type=F32).astype(BF16)
    k_grad = dot_tn(q, score_grad).astype(BF16)
    v_grad = dot_tn(g, low).astype(BF16)
    return q_grad, k_grad, v_grad


MESH = pl.DeviceIdType.MESH
WSLOTS = 5


class Send:
    def __init__(self, src, dst, sems, index, seq, tp):
        send, recv = sems
        self.copy = pltpu.make_async_remote_copy(
            src_ref=src, dst_ref=dst, send_sem=send.at[index], recv_sem=recv.at[index],
            device_id={"seq": seq, "tp": tp}, device_id_type=MESH)

    def start(self):
        self.copy.start()
        return self

    def arrived(self):
        self.copy.wait_recv()

    def left(self):
        self.copy.wait_send()


def kernel(docs, doc_ref, pos_ref, len_ref, off_ref, q_hbm, s_hbm, wk_hbm, wv_hbm, g_hbm,
           qg_out, kw_out, vw_out,
           states, queries, grads, weights, packed, arrived, own, acc, kv, gown, gfar, sfar,
           far_out, far_in, near_out, near_in,
           load_sem, w_sem, a_send, a_recv, b_send, b_recv, c_send, c_recv, d_send, d_recv,
           g_send, g_recv, f_send, f_recv, r_send, r_recv, n_send, n_recv):
    rows = states.shape[0]
    me, tp = lax.axis_index("seq"), lax.axis_index("tp")
    x, z = me // 4, me % 4
    y, core = tp // 2, tp % 2

    def ring(v, k):
        return (v + k % 4) % 4

    def at_x(k):
        return ring(x, k) * 4 + z

    def at_z(k):
        return x * 4 + ring(z, k)

    def at_y(k, c=None):
        return ring(y, k) * 2 + (core if c is None else c)

    other = 1 - core
    partner = y * 2 + other
    line = (at_x, at_z)
    cross = (at_z, at_x)
    spot = (x, z)
    cross_spot = (z, x)

    loads = [pltpu.make_async_copy(s, d, load_sem.at[i])
             for i, (s, d) in enumerate(((s_hbm, states), (q_hbm, queries), (g_hbm, grads)))]
    for load in loads:
        load.start()
    slices = [at_y(0), partner, at_y(-1), at_y(1), at_y(-1, other), at_y(1, other), at_y(2), at_y(2, other)]

    def weight_loads(i):
        slot = i % WSLOTS
        return [pltpu.make_async_copy(w.at[slices[i]], weights.at[slot, p], w_sem.at[slot, p])
                for p, w in enumerate((wk_hbm, wv_hbm))]

    for i in range(WSLOTS):
        for load in weight_loads(i):
            load.start()

    barrier = pltpu.get_barrier_semaphore()
    for k in range(1, docs):
        pl.semaphore_signal(barrier, inc=1, device_id={"seq": (me + k) % docs, "tp": tp}, device_id_type=MESH)
    for t in (at_y(1), at_y(-1), partner):
        pl.semaphore_signal(barrier, inc=1, device_id={"seq": me, "tp": t}, device_id_type=MESH)

    table = pack_table(doc_ref, me, docs, rows)
    loads[0].wait()
    for h in range(2):
        block = jnp.dot(table, states[:, 256 * h:256 * h + 256], preferred_element_type=F32).astype(BF16)
        packed[h] = block.reshape(docs, SLOTS, 256)
    pl.semaphore_wait(barrier, docs - 1 + 3)
    routes = [[], []]
    for h in range(2):
        for k in range(1, docs):
            to = (me + k) % docs
            routes[h].append(Send(packed.at[h, to], arrived.at[h, me], (a_send, a_recv), (h, k), to, tp).start())
        arrived[h, me] = packed[h, me]
    table = order_table(doc_ref, pos_ref, me, docs, rows)

    gather = [{}, {}]
    for h in range(2):
        for route in routes[h]:
            route.arrived()
        own[2 * tp + h] = jnp.dot(table, arrived[h].reshape(docs * SLOTS, 256), preferred_element_type=F32).astype(BF16)
        piece = own.at[2 * tp + h]
        for i, t in enumerate((at_y(1), at_y(-1), partner)):
            gather[h][i] = Send(piece, piece, (b_send, b_recv), (h, i), me, t).start()

    def pass_on(h, i, origin, to):
        piece = own.at[2 * origin + h]
        gather[h][i] = Send(piece, piece, (b_send, b_recv), (h, i), me, to).start()

    def project(i):
        for load in weight_loads(i):
            load.wait()
        slot, part = i % WSLOTS, slices[i]
        last = i == len(slices) - 1

        def step(n, carry):
            p, j = n // 4, n % 4
            cols = pl.ds(pl.multiple_of(j * 256, 256), 256)
            left = jnp.concatenate([own[2 * part], own[2 * part + 1]], axis=1)
            value = jnp.dot(left, weights[slot, p, :, cols], preferred_element_type=F32)
            if i > 0:
                value = acc[p, j, :rows, :] + value
            if last:
                kv[p, :, cols] = value.astype(BF16)
            else:
                acc[p, j, :rows, :] = value
            return carry

        lax.fori_loop(0, 8, step, 0)
        if i + WSLOTS < len(slices):
            for load in weight_loads(i + WSLOTS):
                load.start()

    project(0)
    for h in range(2):
        gather[h][2].arrived()
    project(1)
    gather[0][0].arrived()
    pass_on(0, 3, at_y(-1), at_y(1))
    pass_on(0, 4, at_y(-1), partner)
    gather[0][1].arrived()
    pass_on(0, 5, at_y(1), partner)
    gather[1][1].arrived()
    pass_on(1, 3, at_y(1), at_y(-1))
    pass_on(1, 5, at_y(1), partner)
    gather[1][0].arrived()
    pass_on(1, 4, at_y(-1), partner)
    project(2)
    project(3)
    for h in range(2):
        gather[h][4].arrived()
        gather[h][5].arrived()
    project(4)
    for h in range(2):
        gather[h][3].arrived()
        pass_on(h, 6, at_y(2), partner)
    project(5)
    for h in range(2):
        gather[h][6].arrived()

    mine = pl.ds(pl.multiple_of(tp * 64, 64), 64)

    view = own.reshape(4, 4, rows, 256)

    def wanted(p, k, span):
        return view.at[ring(x, k), :, span, :] if p == 0 else view.at[:, ring(z, k), span, :]

    spread = {}
    for p in range(2):
        for slot, k in ((0, 1), (2, -1), (1, 2)):
            spread[p, slot] = Send(wanted(p, k, mine), sfar.at[p, slot, :, mine, :], (c_send, c_recv), (p, slot),
                                   line[p](k), tp).start()
    project(6)
    project(7)
    for load in loads[1:]:
        load.wait()

    second = {}

    def part_of(p, origin, js=None):
        span = pl.ds(pl.multiple_of(origin * 64, 64), 64)
        return sfar.at[p, :, :, span, :] if js is None else sfar.at[p, :, js, span, :]

    def hand(p, i, origin, to, js=None):
        piece = part_of(p, origin, js)
        second[p, i] = Send(piece, piece, (d_send, d_recv), (p, i), me, to).start()

    def second_own(p):
        for slot in range(3):
            spread[p, slot].arrived()
        for i, t in enumerate((at_y(1), at_y(-1), partner)):
            hand(p, i, tp, t)

    def second_near(p):
        second[p, 0].arrived()
        hand(p, 3, at_y(-1), at_y(1), pl.ds(0, 2))
        hand(p, 4, at_y(-1), partner)
        second[p, 1].arrived()
        hand(p, 7, at_y(1), at_y(-1), pl.ds(2, 2))
        hand(p, 5, at_y(1), partner)

    def second_far(p):
        second[p, 3].arrived()
        second[p, 7].arrived()
        hand(p, 6, at_y(2), partner)

    def second_all(p):
        for i in (2, 4, 5, 6):
            second[p, i].arrived()

    length, offset = len_ref[me], off_ref[me]
    shared = {}
    for chunk in range(4):
        def head(i, carry):
            at = pl.multiple_of((2 * chunk + i) * HEAD_DIM, HEAD_DIM)
            cols = pl.ds(at, HEAD_DIM)
            qg, kg, vg = attention_head(queries[:, cols], kv[0, :, cols], kv[1, :, cols], grads[:, cols], length, offset)
            qg_out[:, cols] = qg
            gown[0, cols, :] = kg
            gown[1, cols, :] = vg
            return carry

        lax.fori_loop(0, 2, head, 0)
        span = pl.ds(256 * chunk, 256)
        for p in range(2):
            for side, (k, slot) in enumerate(((1, 0), (-1, 2))):
                shared[p, chunk, side] = Send(gown.at[p, span, :], gfar.at[p, slot, span, :], (g_send, g_recv),
                                              (p, chunk, side), line[p](k), tp).start()
        if chunk == 2:
            second_own(0)

    passed = {}

    def forward(p, chunk):
        side = 0 if chunk < 2 else 1
        k, slot = ((1, 0), (-1, 2))[side]
        span = pl.ds(256 * chunk, 256)
        shared[p, chunk, side].arrived()
        passed[p, chunk] = Send(gfar.at[p, slot, span, :], gfar.at[p, 1, span, :], (f_send, f_recv), (p, chunk),
                                line[p](k), tp).start()

    def multiply(p, grad, state, first=False):
        def step(n, carry):
            half, j = n // 4, n % 4
            span = pl.ds(pl.multiple_of(half * 512, 512), 512)
            value = jnp.dot(grad[span, :], state(j), preferred_element_type=F32)
            acc[p, j, span, :] = value if first else acc[p, j, span, :] + value
            return carry

        lax.fori_loop(0, 8, step, 0)

    def mine_for(p):
        return (lambda j: own[4 * x + j]) if p == 0 else (lambda j: own[4 * j + z])

    def theirs(p, slot):
        return lambda j: sfar[p, slot, j]

    def near_docs(p):
        for side, slot in ((0, 0), (1, 2)):
            for chunk in range(4):
                if (chunk < 2) != (side == 0):
                    shared[p, chunk, side].arrived()
            multiply(p, gfar.at[p, slot], theirs(p, slot))

    multiply(0, gown.at[0], mine_for(0), True)
    second_near(0)
    second_own(1)
    multiply(1, gown.at[1], mine_for(1), True)
    for p in range(2):
        forward(p, 0)
        forward(p, 1)
    second_far(0)
    second_all(0)
    for p in range(2):
        forward(p, 2)
        forward(p, 3)
    near_docs(0)
    second_near(1)
    second_far(1)
    second_all(1)
    near_docs(1)

    top, bottom = pl.ds(0, 512), pl.ds(512, 512)

    def total(p, k, span):
        j = ring(cross_spot[p], k)
        return acc[p, j, span, :] + jnp.dot(gfar[p, 1, span, :], sfar[p, 1, j], preferred_element_type=F32)

    sums = {}

    def give(p, i, src, dst, k, sems):
        sums[p, i] = Send(src, dst, sems, (p, i), cross[p](k), tp).start()

    for p in range(2):
        for chunk in range(4):
            passed[p, chunk].arrived()
        far_out[p, 0] = total(p, 2, top).astype(BF16)
        far_out[p, 1] = total(p, 2, bottom).astype(BF16)
        give(p, 0, far_out.at[p, 0], far_in.at[p, 0], 1, (r_send, r_recv))
        give(p, 1, far_out.at[p, 1], far_in.at[p, 1], -1, (r_send, r_recv))
    for p in range(2):
        near_out[p, 0, 1] = total(p, 1, bottom).astype(BF16)
        near_out[p, 1, 0] = total(p, -1, top).astype(BF16)
        sums[p, 3] = Send(near_out.at[p, 0, 1], near_in.at[p, 0, 1], (n_send, n_recv), (p, 1), cross[p](1), tp).start()
        sums[p, 4] = Send(near_out.at[p, 1, 0], near_in.at[p, 1, 0], (n_send, n_recv), (p, 2), cross[p](-1), tp).start()
    for p in range(2):
        acc[p, ring(cross_spot[p], 1), top, :] = total(p, 1, top)
        acc[p, ring(cross_spot[p], -1), bottom, :] = total(p, -1, bottom)
    for p in range(2):
        sums[p, 0].arrived()
        near_out[p, 0, 0] = (acc[p, ring(cross_spot[p], 1), top, :] + far_in[p, 0].astype(F32)).astype(BF16)
        sums[p, 2] = Send(near_out.at[p, 0, 0], near_in.at[p, 0, 0], (n_send, n_recv), (p, 0), cross[p](1), tp).start()
        sums[p, 1].arrived()
        near_out[p, 1, 1] = (acc[p, ring(cross_spot[p], -1), bottom, :] + far_in[p, 1].astype(F32)).astype(BF16)
        sums[p, 5] = Send(near_out.at[p, 1, 1], near_in.at[p, 1, 1], (n_send, n_recv), (p, 3), cross[p](-1), tp).start()
    for p in range(2):
        for half, span in enumerate((top, bottom)):
            acc[p, cross_spot[p], span, :] = total(p, 0, span)
    for p, out in enumerate((kw_out, vw_out)):
        for half in (0, 1):
            for i in ((2, 4), (3, 5))[half]:
                sums[p, i].arrived()
            span = pl.ds(512 * half, 512)
            value = (acc[p, cross_spot[p], span, :] + near_in[p, 0, half].astype(F32)) + near_in[p, 1, half].astype(F32)
            out[:, 512 * half:512 * half + 512] = value.T.astype(BF16)

    for group in routes:
        for route in group:
            route.left()
    for group in gather:
        for send in group.values():
            send.left()
    for group in (spread, second, shared, passed, sums):
        for send in group.values():
            send.left()


def shards(queries, states, state_doc, state_pos, lengths, offsets, key_weight, value_weight, context_grad):
    docs = lax.axis_size("seq")
    parts = lax.axis_size("tp")
    rows, features = states.shape
    count, width = queries.shape
    any_spec = pl.BlockSpec(memory_space=pl.ANY)
    vmem_spec = pl.BlockSpec(memory_space=pltpu.VMEM)
    smem_spec = pl.BlockSpec(memory_space=pltpu.SMEM)
    dma = pltpu.SemaphoreType.DMA
    pair = lambda *shape: [dma(shape), dma(shape)]
    return pl.pallas_call(
        functools.partial(kernel, docs),
        out_shape=[jax.ShapeDtypeStruct((count, width), BF16), jax.ShapeDtypeStruct((256, width), BF16),
                   jax.ShapeDtypeStruct((256, width), BF16)],
        in_specs=[vmem_spec, vmem_spec, smem_spec, smem_spec] + [any_spec] * 5,
        out_specs=[vmem_spec] * 3,
        scratch_shapes=[
            pltpu.VMEM((rows, features), BF16),
            pltpu.VMEM((count, width), BF16),
            pltpu.VMEM((count, width), BF16),
            pltpu.VMEM((WSLOTS, 2, features, width), BF16),
            pltpu.VMEM((2, docs, SLOTS, 256), BF16),
            pltpu.VMEM((2, docs, SLOTS, 256), BF16),
            pltpu.VMEM((16, rows, 256), BF16),
            pltpu.VMEM((2, 4, width, 256), F32),
            pltpu.VMEM((2, rows, width), BF16),
            pltpu.VMEM((2, width, rows), BF16),
            pltpu.VMEM((2, 3, width, rows), BF16),
            pltpu.VMEM((2, 3, 4, rows, 256), BF16),
            pltpu.VMEM((2, 2, 512, 256), BF16),
            pltpu.VMEM((2, 2, 512, 256), BF16),
            pltpu.VMEM((2, 2, 2, 512, 256), BF16),
            pltpu.VMEM((2, 2, 2, 512, 256), BF16),
            dma((3,)), dma((WSLOTS, 2)),
            *pair(2, docs), *pair(2, 7), *pair(2, 3), *pair(2, 8),
            *pair(2, 4, 2), *pair(2, 4), *pair(2, 2), *pair(2, 4),
        ],
        compiler_params=pltpu.CompilerParams(collective_id=0, has_side_effects=True, vmem_limit_bytes=67043328),
        name="routed",
    )(state_doc.reshape(-1, 128), state_pos.reshape(-1, 128), lengths, offsets, queries, states,
      key_weight.reshape(parts, features, width), value_weight.reshape(parts, features, width), context_grad)


def solution(mesh):
    in_specs = (P("seq", "tp"), P("seq", "tp"), P(), P(), P(), P(), P(None, "tp"), P(None, "tp"), P("seq", "tp"))
    out_specs = (P("seq", "tp"), P("seq", "tp"), P("seq", "tp"))
    return jax.shard_map(shards, mesh=mesh, in_specs=in_specs, out_specs=out_specs, check_vma=False)
```

time: 233 us -> 124 us (0.53)
  waiting for transfers between devices: 142 us -> 0 us
  Pallas kernels: 12.8 us -> 118 us
  matrix products: 36.4 us -> 0 us
  blocking collectives: 24.2 us -> 0 us
  between operations: 14.1 us -> 0.64 us
  local copies, waits for them, and re-layouts: 2.25 us -> 5.6 us
    reduce_scatter x1 -> x0, waiting for transfers between devices: 110 us -> none  [shards(): summed = lax.psum_scatter(parts, 'seq', scatter_dimension=0, tiled=True)]
    pallas_call x2 -> x1, Pallas kernels: 12.8 us -> 118 us  [shards(): pl.pallas_call(functools.partial(kernel, docs), out_shape=[jax.ShapeDtype...]
    dot_general x5 -> x0, matrix products: 36.4 us -> none  [the longest x1 14.6 us: shards(): lax.dot_general(doc_states, both, (((0,), (1,)), ((), ())), preferred_ele...]
    all_gather x1 -> x0, waiting for transfers between devices: 31.9 us -> none  [shards(): doc_states = lax.all_gather(own, 'tp', axis=1, tiled=True)]
    all_to_all x1 -> x0, blocking collectives: 24.2 us -> none  [shards(): lax.all_to_all(packed, 'seq', split_axis=0, concat_axis=0, tiled=True)]
    unnamed x6 -> x3, local copies, waits for them, and re-layouts: 0.02 us -> 5.6 us
  transfers between devices with their start and end apart: 2 -> 0, of which waited for: 2 -> 0; matrix products, arithmetic and copies ran while one was open for 0% -> 0% of each run, Pallas kernels for 0% -> 0%
where the time goes in v2:
time: 124 us
  Pallas kernels  118 us (95%)
  local copies, waits for them, and re-layouts  5.6 us (5%)
    pallas_call x1, Pallas kernels, shards(): pl.pallas_call(functools.partial(kernel, docs), out_shape=[jax.ShapeDtype...  118 us
    unnamed x3, local copies, waits for them, and re-layouts  5.6 us

profile of v2, /device:TPU:1, one launch (start us, length us, event | category | flops | bytes accessed | tf_op | source)
XLA Modules:
  0.0 124.1 jit_solution(4456380601131673319)
XLA Ops:
  0.6 117.9 %routed.1 = (bf16[256,1024]{1,0:T(8,128)(2,1)}, bf16[256,1024]{1,0:T(8,128)(2,1)}, bf16[256,1024]{1,0:T(8,128)(2,1)}) custom-call(s32[64,128]{1,0:T(8,128)} %bitcast.6, s32[64,128]{1,0:T(8,128)} %bitcast.7, s32[16]{0:T(128)} %len_ref.1, s32[16]{0:T(128)} %off_ref.1, bf16[256,1024]{1,0:T(8,128)(2,1)} %q_hbm.1, bf16[512,512]{1,0:T(8,128)(2,1)} %s_hbm.1, ...), custom_call_target="tpu_custom_call" | custom-call | tf_op jit(solution)/shard_map/routed/pallas_call | solution.py:417
  118.5 1.9 %copy.15 = bf16[256,1024]{1,0:T(8,128)(2,1)} copy(bf16[256,1024]{1,0:T(8,128)(2,1)} %get-tuple-element.6) | data formatting | bytes 1048576
  120.4 1.9 %copy.16 = bf16[256,1024]{1,0:T(8,128)(2,1)} copy(bf16[256,1024]{1,0:T(8,128)(2,1)} %get-tuple-element.7) | data formatting | bytes 1048576
  122.2 1.9 %copy.17 = bf16[256,1024]{1,0:T(8,128)(2,1)} copy(bf16[256,1024]{1,0:T(8,128)(2,1)} %get-tuple-element.8) | data formatting | bytes 1048576

commit v3 on v2

--- a/solution.py
+++ b/solution.py
@@ -78,6 +78,7 @@
 
 MESH = pl.DeviceIdType.MESH
 WSLOTS = 5
+STARTED = []
 
 
 class Send:
@@ -86,15 +87,20 @@
         self.copy = pltpu.make_async_remote_copy(
             src_ref=src, dst_ref=dst, send_sem=send.at[index], recv_sem=recv.at[index],
             device_id={"seq": seq, "tp": tp}, device_id_type=MESH)
+        self.waited = False
 
     def start(self):
         self.copy.start()
+        STARTED.append(self)
         return self
 
     def arrived(self):
         self.copy.wait_recv()
-
-    def left(self):
+        self.waited = True
+
+    def finish(self):
+        if not self.waited:
+            self.arrived()
         self.copy.wait_send()
 
 
@@ -104,6 +110,12 @@
            far_out, far_in, near_out, near_in,
            load_sem, w_sem, a_send, a_recv, b_send, b_recv, c_send, c_recv, d_send, d_recv,
            g_send, g_recv, f_send, f_recv, r_send, r_recv, n_send, n_recv):
+    STARTED.clear()
+
+    def drain():
+        for send in STARTED:
+            send.finish()
+
     rows = states.shape[0]
     me, tp = lax.axis_index("seq"), lax.axis_index("tp")
     x, z = me // 4, me % 4
@@ -183,19 +195,22 @@
         last = i == len(slices) - 1
 
         def step(n, carry):
-            p, j = n // 4, n % 4
-            cols = pl.ds(pl.multiple_of(j * 256, 256), 256)
             left = jnp.concatenate([own[2 * part], own[2 * part + 1]], axis=1)
+            p, m = n // (1024 // 1024), n % (1024 // 1024)
+            cols = pl.ds(pl.multiple_of(m * 1024, 1024), 1024)
             value = jnp.dot(left, weights[slot, p, :, cols], preferred_element_type=F32)
-            if i > 0:
-                value = acc[p, j, :rows, :] + value
-            if last:
-                kv[p, :, cols] = value.astype(BF16)
-            else:
-                acc[p, j, :rows, :] = value
+            for b in range(1024 // 256):
+                j = m * (1024 // 256) + b
+                v = value[:, 256 * b:256 * b + 256]
+                if i > 0:
+                    v = acc[p, j, :rows, :] + v
+                if last:
+                    kv[p, :, pl.ds(pl.multiple_of(j * 256, 256), 256)] = v.astype(BF16)
+                else:
+                    acc[p, j, :rows, :] = v
             return carry
 
-        lax.fori_loop(0, 8, step, 0)
+        lax.fori_loop(0, 2, step, 0)
         if i + WSLOTS < len(slices):
             for load in weight_loads(i + WSLOTS):
                 load.start()
@@ -295,8 +310,9 @@
             for side, (k, slot) in enumerate(((1, 0), (-1, 2))):
                 shared[p, chunk, side] = Send(gown.at[p, span, :], gfar.at[p, slot, span, :], (g_send, g_recv),
                                               (p, chunk, side), line[p](k), tp).start()
-        if chunk == 2:
+        if chunk == 0:
             second_own(0)
+            second_own(1)
 
     passed = {}
 
@@ -309,14 +325,12 @@
                                 line[p](k), tp).start()
 
     def multiply(p, grad, state, first=False):
-        def step(n, carry):
-            half, j = n // 4, n % 4
-            span = pl.ds(pl.multiple_of(half * 512, 512), 512)
-            value = jnp.dot(grad[span, :], state(j), preferred_element_type=F32)
-            acc[p, j, span, :] = value if first else acc[p, j, span, :] + value
+        def step(j, carry):
+            value = jnp.dot(grad[...], state(j), preferred_element_type=F32)
+            acc[p, j] = value if first else acc[p, j] + value
             return carry
 
-        lax.fori_loop(0, 8, step, 0)
+        lax.fori_loop(0, 4, step, 0)
 
     def mine_for(p):
         return (lambda j: own[4 * x + j]) if p == 0 else (lambda j: own[4 * j + z])
@@ -333,18 +347,17 @@
 
     multiply(0, gown.at[0], mine_for(0), True)
     second_near(0)
-    second_own(1)
     multiply(1, gown.at[1], mine_for(1), True)
     for p in range(2):
         forward(p, 0)
         forward(p, 1)
+    second_near(1)
+    for p in range(2):
+        forward(p, 2)
+        forward(p, 3)
     second_far(0)
     second_all(0)
-    for p in range(2):
-        forward(p, 2)
-        forward(p, 3)
     near_docs(0)
-    second_near(1)
     second_far(1)
     second_all(1)
     near_docs(1)
@@ -393,15 +406,12 @@
             value = (acc[p, cross_spot[p], span, :] + near_in[p, 0, half].astype(F32)) + near_in[p, 1, half].astype(F32)
             out[:, 512 * half:512 * half + 512] = value.T.astype(BF16)
 
-    for group in routes:
-        for route in group:
-            route.left()
-    for group in gather:
-        for send in group.values():
-            send.left()
-    for group in (spread, second, shared, passed, sums):
-        for send in group.values():
-            send.left()
+    drain()
+
+
+def hand_over(*refs):
+    for source, target in zip(refs[:3], refs[3:]):
+        target[...] = source[...]
 
 
 def shards(queries, states, state_doc, state_pos, lengths, offsets, key_weight, value_weight, context_grad):
@@ -414,7 +424,7 @@
     smem_spec = pl.BlockSpec(memory_space=pltpu.SMEM)
     dma = pltpu.SemaphoreType.DMA
     pair = lambda *shape: [dma(shape), dma(shape)]
-    return pl.pallas_call(
+    results = pl.pallas_call(
         functools.partial(kernel, docs),
         out_shape=[jax.ShapeDtypeStruct((count, width), BF16), jax.ShapeDtypeStruct((256, width), BF16),
                    jax.ShapeDtypeStruct((256, width), BF16)],
@@ -445,6 +455,15 @@
         name="routed",
     )(state_doc.reshape(-1, 128), state_pos.reshape(-1, 128), lengths, offsets, queries, states,
       key_weight.reshape(parts, features, width), value_weight.reshape(parts, features, width), context_grad)
+    block = pl.BlockSpec((64, width), lambda i: (i, 0))
+    return pl.pallas_call(
+        hand_over,
+        grid=(4,),
+        out_shape=[jax.ShapeDtypeStruct((256, width), BF16)] * 3,
+        in_specs=[block] * 3,
+        out_specs=[block] * 3,
+        name="hand_over",
+    )(*results)
 
 
 def solution(mesh):

time: 124 us -> 113 us (0.911)
  Pallas kernels: 118 us -> 111 us
  local copies, waits for them, and re-layouts: 5.6 us -> 0 us
    pallas_call x1, Pallas kernels: 118 us -> 108 us  [shards(): pl.pallas_call(functools.partial(kernel, docs), out_shape=[jax.ShapeDtype...]
    unnamed x3 -> x0, local copies, waits for them, and re-layouts: 5.6 us -> none
    pallas_call x0 -> x1, Pallas kernels: none -> 3.62 us  [shards(): pl.pallas_call(hand_over, grid=(4,), out_shape=[jax.ShapeDtypeStruct((256...]
where the time goes in v3:
time: 113 us; the launch traced here: 112 us
  Pallas kernels  111 us (98%)
    pallas_call x1, Pallas kernels, shards(): pl.pallas_call(functools.partial(kernel, docs), out_shape=[jax.ShapeDtype...  108 us
    pallas_call x1, Pallas kernels, shards(): pl.pallas_call(hand_over, grid=(4,), out_shape=[jax.ShapeDtypeStruct((256...  3.62 us

profile of v3, /device:TPU:1, one launch (start us, length us, event | category | flops | bytes accessed | tf_op | source)
XLA Modules:
  0.0 111.9 jit_solution(17499222495731913551)
XLA Ops:
  0.6 107.6 %routed.1 = (bf16[256,1024]{1,0:T(8,128)(2,1)}, bf16[256,1024]{1,0:T(8,128)(2,1)}, bf16[256,1024]{1,0:T(8,128)(2,1)}) custom-call(s32[64,128]{1,0:T(8,128)} %bitcast.6, s32[64,128]{1,0:T(8,128)} %bitcast.7, s32[16]{0:T(128)} %len_ref.1, s32[16]{0:T(128)} %off_ref.1, bf16[256,1024]{1,0:T(8,128)(2,1)} %q_hbm.1, bf16[512,512]{1,0:T(8,128)(2,1)} %s_hbm.1, ...), custom_call_target="tpu_custom_call" | custom-call | tf_op jit(solution)/shard_map/routed/pallas_call | solution.py:427
  108.3 3.6 %hand_over.1 = (bf16[256,1024]{1,0:T(8,128)(2,1)}, bf16[256,1024]{1,0:T(8,128)(2,1)}, bf16[256,1024]{1,0:T(8,128)(2,1)}) custom-call(bf16[256,1024]{1,0:T(8,128)(2,1)} %get-tuple-element.6.refs_0_, bf16[256,1024]{1,0:T(8,128)(2,1)} %get-tuple-element.7.refs_1_, bf16[256,1024]{1,0:T(8,128)(2,1)} %get-tuple-element.8.refs_2_), custom_call_target="tpu_custom_call" | custom-call | tf_op jit(solution)/shard_map/hand_over/pallas_call | solution.py:459

commit v4 on v3

--- a/solution.py
+++ b/solution.py
@@ -9,6 +9,7 @@
 
 HEAD_DIM = 128
 SLOTS = 64
+USED = 56
 F32 = jnp.float32
 BF16 = jnp.bfloat16
 
@@ -144,7 +145,7 @@
              for i, (s, d) in enumerate(((s_hbm, states), (q_hbm, queries), (g_hbm, grads)))]
     for load in loads:
         load.start()
-    slices = [at_y(0), partner, at_y(-1), at_y(1), at_y(-1, other), at_y(1, other), at_y(2), at_y(2, other)]
+    slices = [at_y(0), partner, at_y(-1), at_y(1), at_y(-1, other), at_y(1, other), at_y(2, 0), at_y(2, 1)]
 
     def weight_loads(i):
         slot = i % WSLOTS
@@ -154,6 +155,8 @@
     for i in range(WSLOTS):
         for load in weight_loads(i):
             load.start()
+
+    arrived[:, :, 48:, :] = jnp.zeros((4, docs, SLOTS - 48, 128), BF16)
 
     barrier = pltpu.get_barrier_semaphore()
     for k in range(1, docs):
@@ -165,34 +168,62 @@
     loads[0].wait()
     for h in range(2):
         block = jnp.dot(table, states[:, 256 * h:256 * h + 256], preferred_element_type=F32).astype(BF16)
-        packed[h] = block.reshape(docs, SLOTS, 256)
+        packed[2 * h] = block[:, :128].reshape(docs, SLOTS, 128)
+        packed[2 * h + 1] = block[:, 128:].reshape(docs, SLOTS, 128)
     pl.semaphore_wait(barrier, docs - 1 + 3)
-    routes = [[], []]
-    for h in range(2):
+    routes = [[], [], [], []]
+    for q in range(4):
         for k in range(1, docs):
             to = (me + k) % docs
-            routes[h].append(Send(packed.at[h, to], arrived.at[h, me], (a_send, a_recv), (h, k), to, tp).start())
-        arrived[h, me] = packed[h, me]
+            routes[q].append(Send(packed.at[q, to, pl.ds(0, USED)], arrived.at[q, me, pl.ds(0, USED)], (a_send, a_recv),
+                                  (q, k), to, tp).start())
+        arrived[q, me] = packed[q, me]
     table = order_table(doc_ref, pos_ref, me, docs, rows)
 
-    gather = [{}, {}]
-    for h in range(2):
-        for route in routes[h]:
+    gather = [{}, {}, {}, {}]
+
+    def pass_on(q, i, origin, to):
+        piece = own.at[2 * origin + q // 2, :, pl.ds(128 * (q % 2), 128)]
+        gather[q][i] = Send(piece, piece, (b_send, b_recv), (q, i), me, to).start()
+
+    for q in range(4):
+        for route in routes[q]:
             route.arrived()
-        own[2 * tp + h] = jnp.dot(table, arrived[h].reshape(docs * SLOTS, 256), preferred_element_type=F32).astype(BF16)
-        piece = own.at[2 * tp + h]
+        value = jnp.dot(table, arrived[q].reshape(docs * SLOTS, 128), preferred_element_type=F32)
+        own[2 * tp + q // 2, :, 128 * (q % 2):128 * (q % 2) + 128] = value.astype(BF16)
         for i, t in enumerate((at_y(1), at_y(-1), partner)):
-            gather[h][i] = Send(piece, piece, (b_send, b_recv), (h, i), me, t).start()
-
-    def pass_on(h, i, origin, to):
-        piece = own.at[2 * origin + h]
-        gather[h][i] = Send(piece, piece, (b_send, b_recv), (h, i), me, to).start()
+            pass_on(q, i, tp, t)
+
+    mine = pl.ds(pl.multiple_of(tp * 64, 64), 64)
+
+    def line_copy(p, k, src, js, to):
+        return pltpu.make_async_remote_copy(
+            src_ref=src, dst_ref=sfar.at[p, k - 1, js, mine, :], send_sem=c_send.at[p, k - 1], recv_sem=c_recv.at[p, k - 1],
+            device_id={"seq": to, "tp": tp}, device_id_type=MESH)
+
+    def spread(part):
+        k = (part // 2 + 4 - x) % 4
+
+        @pl.when(k != 0)
+        def _():
+            line_copy(0, k, own.at[pl.ds(2 * part, 2), mine, :], pl.ds(2 * (part % 2), 2), (part // 2) * 4 + z).start()
+
+        for h in range(2):
+            block = 2 * part + h
+            l = (block % 4 + 4 - z) % 4
+
+            @pl.when(l != 0)
+            def _(block=block, l=l):
+                line_copy(1, l, own.at[pl.ds(block, 1), mine, :], pl.ds(block // 4, 1), x * 4 + block % 4).start()
+
+    def spread_all(p, slot):
+        to = line[p](slot + 1)
+        return line_copy(p, slot + 1, sfar.at[p, slot, :, mine, :], slice(None), to)
 
     def project(i):
         for load in weight_loads(i):
             load.wait()
         slot, part = i % WSLOTS, slices[i]
-        last = i == len(slices) - 1
 
         def step(n, carry):
             left = jnp.concatenate([own[2 * part], own[2 * part + 1]], axis=1)
@@ -204,10 +235,7 @@
                 v = value[:, 256 * b:256 * b + 256]
                 if i > 0:
                     v = acc[p, j, :rows, :] + v
-                if last:
-                    kv[p, :, pl.ds(pl.multiple_of(j * 256, 256), 256)] = v.astype(BF16)
-                else:
-                    acc[p, j, :rows, :] = v
+                acc[p, j, :rows, :] = v
             return carry
 
         lax.fori_loop(0, 2, step, 0)
@@ -215,49 +243,44 @@
             for load in weight_loads(i + WSLOTS):
                 load.start()
 
+    spread(tp)
     project(0)
-    for h in range(2):
-        gather[h][2].arrived()
+    for q in range(4):
+        gather[q][2].arrived()
+    spread(partner)
     project(1)
-    gather[0][0].arrived()
-    pass_on(0, 3, at_y(-1), at_y(1))
-    pass_on(0, 4, at_y(-1), partner)
-    gather[0][1].arrived()
-    pass_on(0, 5, at_y(1), partner)
-    gather[1][1].arrived()
-    pass_on(1, 3, at_y(1), at_y(-1))
-    pass_on(1, 5, at_y(1), partner)
-    gather[1][0].arrived()
-    pass_on(1, 4, at_y(-1), partner)
+    for q in range(4):
+        gather[q][0].arrived()
+        if q < 2:
+            pass_on(q, 3, at_y(-1), at_y(1))
+        pass_on(q, 4, at_y(-1), partner)
+        gather[q][1].arrived()
+        if q >= 2:
+            pass_on(q, 3, at_y(1), at_y(-1))
+        pass_on(q, 5, at_y(1), partner)
+    spread(at_y(-1))
+    spread(at_y(1))
     project(2)
     project(3)
-    for h in range(2):
-        gather[h][4].arrived()
-        gather[h][5].arrived()
+    for q in range(4):
+        gather[q][4].arrived()
+        gather[q][5].arrived()
+    spread(at_y(-1, other))
+    spread(at_y(1, other))
     project(4)
-    for h in range(2):
-        gather[h][3].arrived()
-        pass_on(h, 6, at_y(2), partner)
+    for q in range(4):
+        gather[q][3].arrived()
+        pass_on(q, 6, at_y(2), partner)
+    spread(at_y(2))
     project(5)
-    for h in range(2):
-        gather[h][6].arrived()
-
-    mine = pl.ds(pl.multiple_of(tp * 64, 64), 64)
-
-    view = own.reshape(4, 4, rows, 256)
-
-    def wanted(p, k, span):
-        return view.at[ring(x, k), :, span, :] if p == 0 else view.at[:, ring(z, k), span, :]
-
-    spread = {}
-    for p in range(2):
-        for slot, k in ((0, 1), (2, -1), (1, 2)):
-            spread[p, slot] = Send(wanted(p, k, mine), sfar.at[p, slot, :, mine, :], (c_send, c_recv), (p, slot),
-                                   line[p](k), tp).start()
-    project(6)
-    project(7)
+    for q in range(4):
+        gather[q][6].arrived()
+    spread(at_y(2, other))
     for load in loads[1:]:
         load.wait()
+    for i in (6, 7):
+        for load in weight_loads(i):
+            load.wait()
 
     second = {}
 
@@ -271,7 +294,7 @@
 
     def second_own(p):
         for slot in range(3):
-            spread[p, slot].arrived()
+            spread_all(p, slot).wait_recv()
         for i, t in enumerate((at_y(1), at_y(-1), partner)):
             hand(p, i, tp, t)
 
@@ -294,7 +317,14 @@
 
     length, offset = len_ref[me], off_ref[me]
     shared = {}
+    view = own.reshape(4, 4, rows, 256)
     for chunk in range(4):
+        last = jnp.concatenate([view[ring(y, 2), b] for b in range(4)], axis=1)
+        for p in range(2):
+            part = weights[6 - WSLOTS:8 - WSLOTS, p, :, 256 * chunk:256 * chunk + 256].reshape(4 * 256, 256)
+            value = acc[p, chunk, :rows, :] + jnp.dot(last, part, preferred_element_type=F32)
+            kv[p, :, 256 * chunk:256 * chunk + 256] = value.astype(BF16)
+
         def head(i, carry):
             at = pl.multiple_of((2 * chunk + i) * HEAD_DIM, HEAD_DIM)
             cols = pl.ds(at, HEAD_DIM)
@@ -314,6 +344,7 @@
             second_own(0)
             second_own(1)
 
+
     passed = {}
 
     def forward(p, chunk):
@@ -361,6 +392,7 @@
     second_far(1)
     second_all(1)
     near_docs(1)
+
 
     top, bottom = pl.ds(0, 512), pl.ds(512, 512)
 
@@ -406,12 +438,18 @@
             value = (acc[p, cross_spot[p], span, :] + near_in[p, 0, half].astype(F32)) + near_in[p, 1, half].astype(F32)
             out[:, 512 * half:512 * half + 512] = value.T.astype(BF16)
 
+    for p in range(2):
+        for slot in range(3):
+            spread_all(p, slot).wait_send()
     drain()
 
 
 def hand_over(*refs):
-    for source, target in zip(refs[:3], refs[3:]):
-        target[...] = source[...]
+    copies = [pltpu.make_async_copy(refs[i], refs[3 + i], refs[6].at[i]) for i in range(3)]
+    for copy in copies:
+        copy.start()
+    for copy in copies:
+        copy.wait()
 
 
 def shards(queries, states, state_doc, state_pos, lengths, offsets, key_weight, value_weight, context_grad):
@@ -426,8 +464,7 @@
     pair = lambda *shape: [dma(shape), dma(shape)]
     results = pl.pallas_call(
         functools.partial(kernel, docs),
-        out_shape=[jax.ShapeDtypeStruct((count, width), BF16), jax.ShapeDtypeStruct((256, width), BF16),
-                   jax.ShapeDtypeStruct((256, width), BF16)],
+        out_shape=[pltpu.VMEM((count, width), BF16)] + [pltpu.VMEM((256, width), BF16)] * 2,
         in_specs=[vmem_spec, vmem_spec, smem_spec, smem_spec] + [any_spec] * 5,
         out_specs=[vmem_spec] * 3,
         scratch_shapes=[
@@ -435,8 +472,8 @@
             pltpu.VMEM((count, width), BF16),
             pltpu.VMEM((count, width), BF16),
             pltpu.VMEM((WSLOTS, 2, features, width), BF16),
-            pltpu.VMEM((2, docs, SLOTS, 256), BF16),
-            pltpu.VMEM((2, docs, SLOTS, 256), BF16),
+            pltpu.VMEM((4, docs, SLOTS, 128), BF16),
+            pltpu.VMEM((4, docs, SLOTS, 128), BF16),
             pltpu.VMEM((16, rows, 256), BF16),
             pltpu.VMEM((2, 4, width, 256), F32),
             pltpu.VMEM((2, rows, width), BF16),
@@ -448,20 +485,20 @@
             pltpu.VMEM((2, 2, 2, 512, 256), BF16),
             pltpu.VMEM((2, 2, 2, 512, 256), BF16),
             dma((3,)), dma((WSLOTS, 2)),
-            *pair(2, docs), *pair(2, 7), *pair(2, 3), *pair(2, 8),
+            *pair(4, docs), *pair(4, 7), *pair(2, 3), *pair(2, 8),
             *pair(2, 4, 2), *pair(2, 4), *pair(2, 2), *pair(2, 4),
         ],
-        compiler_params=pltpu.CompilerParams(collective_id=0, has_side_effects=True, vmem_limit_bytes=67043328),
+        compiler_params=pltpu.CompilerParams(collective_id=0, has_side_effects=True, vmem_limit_bytes=60 << 20),
         name="routed",
     )(state_doc.reshape(-1, 128), state_pos.reshape(-1, 128), lengths, offsets, queries, states,
       key_weight.reshape(parts, features, width), value_weight.reshape(parts, features, width), context_grad)
-    block = pl.BlockSpec((64, width), lambda i: (i, 0))
     return pl.pallas_call(
         hand_over,
-        grid=(4,),
         out_shape=[jax.ShapeDtypeStruct((256, width), BF16)] * 3,
-        in_specs=[block] * 3,
-        out_specs=[block] * 3,
+        in_specs=[vmem_spec] * 3,
+        out_specs=[any_spec] * 3,
+        scratch_shapes=[dma((3,))],
+        compiler_params=pltpu.CompilerParams(vmem_limit_bytes=4 << 20),
         name="hand_over",
     )(*results)
 

time: 113 us -> 102 us (0.903)
  Pallas kernels: 111 us -> 100 us
    pallas_call x2, Pallas kernels: 111 us -> 100 us  [the longest x1 99.2 us: shards(): pl.pallas_call(functools.partial(kernel, docs), out_shape=[pltpu.VMEM((co...]
where the time goes in v4:
time: 102 us; the launch traced here: 101 us
  Pallas kernels  100 us (98%)
    pallas_call x1, Pallas kernels, shards(): pl.pallas_call(functools.partial(kernel, docs), out_shape=[pltpu.VMEM((co...  99.2 us

profile of v4, /device:TPU:1, one launch (start us, length us, event | category | flops | bytes accessed | tf_op | source)
XLA Modules:
  0.0 101.2 jit_solution(1582998906375145078)
XLA Ops:
  0.6 99.2 %routed.1 = (bf16[256,1024]{1,0:T(8,128)(2,1)S(1)}, bf16[256,1024]{1,0:T(8,128)(2,1)S(1)}, bf16[256,1024]{1,0:T(8,128)(2,1)S(1)}) custom-call(s32[64,128]{1,0:T(8,128)} %bitcast.6, s32[64,128]{1,0:T(8,128)} %bitcast.7, s32[16]{0:T(128)} %len_ref.1, s32[16]{0:T(128)} %off_ref.1, bf16[256,1024]{1,0:T(8,128)(2,1)} %q_hbm.1, bf16[512,512]{1,0:T(8,128)(2,1)} %s_hbm.1, ...), custom_call_target="tpu_custom_call" | custom-call | tf_op jit(solution)/shard_map/routed/pallas_call | solution.py:465
  99.8 1.2 %hand_over.1 = (bf16[256,1024]{1,0:T(8,128)(2,1)}, bf16[256,1024]{1,0:T(8,128)(2,1)}, bf16[256,1024]{1,0:T(8,128)(2,1)}) custom-call(bf16[256,1024]{1,0:T(8,128)(2,1)S(1)} %get-tuple-element.6.refs_0_, bf16[256,1024]{1,0:T(8,128)(2,1)S(1)} %get-tuple-element.7.refs_1_, bf16[256,1024]{1,0:T(8,128)(2,1)S(1)} %get-tuple-element.8.refs_2_), custom_call_target="tpu_custom_call" | custom-call | tf_op jit(solution)/shard_map/hand_over/pallas_call | solution.py:495

commit v5 on v4

--- a/solution.py
+++ b/solution.py
@@ -171,10 +171,11 @@
         packed[2 * h] = block[:, :128].reshape(docs, SLOTS, 128)
         packed[2 * h + 1] = block[:, 128:].reshape(docs, SLOTS, 128)
     pl.semaphore_wait(barrier, docs - 1 + 3)
+    peers = sorted(((i, j) for i in range(4) for j in range(4) if i or j), key=lambda d: min(d[0], 4 - d[0]) + min(d[1], 4 - d[1]))
     routes = [[], [], [], []]
     for q in range(4):
-        for k in range(1, docs):
-            to = (me + k) % docs
+        for k, (i, j) in enumerate(peers):
+            to = ring(x, i) * 4 + ring(z, j)
             routes[q].append(Send(packed.at[q, to, pl.ds(0, USED)], arrived.at[q, me, pl.ds(0, USED)], (a_send, a_recv),
                                   (q, k), to, tp).start())
         arrived[q, me] = packed[q, me]
@@ -325,21 +326,16 @@
             value = acc[p, chunk, :rows, :] + jnp.dot(last, part, preferred_element_type=F32)
             kv[p, :, 256 * chunk:256 * chunk + 256] = value.astype(BF16)
 
-        def head(i, carry):
-            at = pl.multiple_of((2 * chunk + i) * HEAD_DIM, HEAD_DIM)
-            cols = pl.ds(at, HEAD_DIM)
+        for piece in (2 * chunk, 2 * chunk + 1):
+            cols = pl.ds(HEAD_DIM * piece, HEAD_DIM)
             qg, kg, vg = attention_head(queries[:, cols], kv[0, :, cols], kv[1, :, cols], grads[:, cols], length, offset)
             qg_out[:, cols] = qg
             gown[0, cols, :] = kg
             gown[1, cols, :] = vg
-            return carry
-
-        lax.fori_loop(0, 2, head, 0)
-        span = pl.ds(256 * chunk, 256)
-        for p in range(2):
-            for side, (k, slot) in enumerate(((1, 0), (-1, 2))):
-                shared[p, chunk, side] = Send(gown.at[p, span, :], gfar.at[p, slot, span, :], (g_send, g_recv),
-                                              (p, chunk, side), line[p](k), tp).start()
+            for p in range(2):
+                for side, (k, slot) in enumerate(((1, 0), (-1, 2))):
+                    shared[p, piece, side] = Send(gown.at[p, cols, :], gfar.at[p, slot, cols, :], (g_send, g_recv),
+                                                  (p, piece, side), line[p](k), tp).start()
         if chunk == 0:
             second_own(0)
             second_own(1)
@@ -347,13 +343,15 @@
 
     passed = {}
 
-    def forward(p, chunk):
-        side = 0 if chunk < 2 else 1
-        k, slot = ((1, 0), (-1, 2))[side]
-        span = pl.ds(256 * chunk, 256)
-        shared[p, chunk, side].arrived()
-        passed[p, chunk] = Send(gfar.at[p, slot, span, :], gfar.at[p, 1, span, :], (f_send, f_recv), (p, chunk),
-                                line[p](k), tp).start()
+    def forward(*pieces):
+        for piece in pieces:
+            side = 0 if piece < 4 else 1
+            k, slot = ((1, 0), (-1, 2))[side]
+            span = pl.ds(HEAD_DIM * piece, HEAD_DIM)
+            for p in range(2):
+                shared[p, piece, side].arrived()
+                passed[p, piece] = Send(gfar.at[p, slot, span, :], gfar.at[p, 1, span, :], (f_send, f_recv), (p, piece),
+                                        line[p](k), tp).start()
 
     def multiply(p, grad, state, first=False):
         def step(j, carry):
@@ -369,74 +367,92 @@
     def theirs(p, slot):
         return lambda j: sfar[p, slot, j]
 
-    def near_docs(p):
-        for side, slot in ((0, 0), (1, 2)):
-            for chunk in range(4):
-                if (chunk < 2) != (side == 0):
-                    shared[p, chunk, side].arrived()
-            multiply(p, gfar.at[p, slot], theirs(p, slot))
+    def near_grads(p):
+        for side in range(2):
+            for piece in range(8):
+                if (piece < 4) != (side == 0):
+                    shared[p, piece, side].arrived()
+
+    def near_block(p, k):
+        j = ring(cross_spot[p], k)
+
+        def step(half, carry):
+            span = pl.ds(pl.multiple_of(half * 512, 512), 512)
+            value = jnp.dot(gfar[p, 0, span, :], sfar[p, 0, j], preferred_element_type=F32)
+            value = value + jnp.dot(gfar[p, 2, span, :], sfar[p, 2, j], preferred_element_type=F32)
+            acc[p, j, span, :] = acc[p, j, span, :] + value
+            return carry
+
+        lax.fori_loop(0, 2, step, 0)
 
     multiply(0, gown.at[0], mine_for(0), True)
     second_near(0)
     multiply(1, gown.at[1], mine_for(1), True)
-    for p in range(2):
-        forward(p, 0)
-        forward(p, 1)
+    forward(0, 1, 2, 3, 4, 5)
     second_near(1)
-    for p in range(2):
-        forward(p, 2)
-        forward(p, 3)
+    forward(6, 7)
     second_far(0)
     second_all(0)
-    near_docs(0)
+    near_grads(0)
+    for k in (2, 1, -1):
+        near_block(0, k)
     second_far(1)
     second_all(1)
-    near_docs(1)
-
-
-    top, bottom = pl.ds(0, 512), pl.ds(512, 512)
-
-    def total(p, k, span):
-        j = ring(cross_spot[p], k)
+    near_grads(1)
+    near_block(1, 2)
+
+
+    def total(p, k, c):
+        j, span = ring(cross_spot[p], k), pl.ds(256 * c, 256)
         return acc[p, j, span, :] + jnp.dot(gfar[p, 1, span, :], sfar[p, 1, j], preferred_element_type=F32)
 
     sums = {}
-
-    def give(p, i, src, dst, k, sems):
-        sums[p, i] = Send(src, dst, sems, (p, i), cross[p](k), tp).start()
-
+    toward = (1, 1, -1, -1)
+
+    def give_near(p, k, c):
+        side = 0 if k == 1 else 1
+        sums[p, side, c] = Send(near_out.at[p, side, c], near_in.at[p, side, c], (n_send, n_recv), (p, 4 * side + c),
+                                cross[p](k), tp).start()
+
+    orders = ((0, 2), (1, 3))
+    for order in orders:
+        for p in range(2):
+            for c in order:
+                passed[p, 2 * c].arrived()
+                passed[p, 2 * c + 1].arrived()
+                far_out[p, c] = total(p, 2, c).astype(BF16)
+                sums[p, c] = Send(far_out.at[p, c], far_in.at[p, c], (r_send, r_recv), (p, c), cross[p](toward[c]), tp).start()
+        for p in range(2):
+            if order == orders[0] and p == 1:
+                near_block(1, 1)
+                near_block(1, -1)
+            for c in order:
+                near_out[p, (1 + toward[c]) // 2, c] = total(p, -toward[c], c).astype(BF16)
+                give_near(p, -toward[c], c)
+    for order in orders:
+        for p in range(2):
+            for c in order:
+                acc[p, ring(cross_spot[p], toward[c]), pl.ds(256 * c, 256), :] = total(p, toward[c], c)
+    for order in orders:
+        for p in range(2):
+            for c in order:
+                k = toward[c]
+                sums[p, c].arrived()
+                value = acc[p, ring(cross_spot[p], k), pl.ds(256 * c, 256), :] + far_in[p, c].astype(F32)
+                near_out[p, (1 - k) // 2, c] = value.astype(BF16)
+                give_near(p, k, c)
     for p in range(2):
-        for chunk in range(4):
-            passed[p, chunk].arrived()
-        far_out[p, 0] = total(p, 2, top).astype(BF16)
-        far_out[p, 1] = total(p, 2, bottom).astype(BF16)
-        give(p, 0, far_out.at[p, 0], far_in.at[p, 0], 1, (r_send, r_recv))
-        give(p, 1, far_out.at[p, 1], far_in.at[p, 1], -1, (r_send, r_recv))
-    for p in range(2):
-        near_out[p, 0, 1] = total(p, 1, bottom).astype(BF16)
-        near_out[p, 1, 0] = total(p, -1, top).astype(BF16)
-        sums[p, 3] = Send(near_out.at[p, 0, 1], near_in.at[p, 0, 1], (n_send, n_recv), (p, 1), cross[p](1), tp).start()
-        sums[p, 4] = Send(near_out.at[p, 1, 0], near_in.at[p, 1, 0], (n_send, n_recv), (p, 2), cross[p](-1), tp).start()
-    for p in range(2):
-        acc[p, ring(cross_spot[p], 1), top, :] = total(p, 1, top)
-        acc[p, ring(cross_spot[p], -1), bottom, :] = total(p, -1, bottom)
-    for p in range(2):
-        sums[p, 0].arrived()
-        near_out[p, 0, 0] = (acc[p, ring(cross_spot[p], 1), top, :] + far_in[p, 0].astype(F32)).astype(BF16)
-        sums[p, 2] = Send(near_out.at[p, 0, 0], near_in.at[p, 0, 0], (n_send, n_recv), (p, 0), cross[p](1), tp).start()
-        sums[p, 1].arrived()
-        near_out[p, 1, 1] = (acc[p, ring(cross_spot[p], -1), bottom, :] + far_in[p, 1].astype(F32)).astype(BF16)
-        sums[p, 5] = Send(near_out.at[p, 1, 1], near_in.at[p, 1, 1], (n_send, n_recv), (p, 3), cross[p](-1), tp).start()
-    for p in range(2):
-        for half, span in enumerate((top, bottom)):
-            acc[p, cross_spot[p], span, :] = total(p, 0, span)
-    for p, out in enumerate((kw_out, vw_out)):
-        for half in (0, 1):
-            for i in ((2, 4), (3, 5))[half]:
-                sums[p, i].arrived()
-            span = pl.ds(512 * half, 512)
-            value = (acc[p, cross_spot[p], span, :] + near_in[p, 0, half].astype(F32)) + near_in[p, 1, half].astype(F32)
-            out[:, 512 * half:512 * half + 512] = value.T.astype(BF16)
+        near_block(p, 0)
+        for c in range(4):
+            acc[p, cross_spot[p], pl.ds(256 * c, 256), :] = total(p, 0, c)
+    for order in orders:
+        for p, out in enumerate((kw_out, vw_out)):
+            for c in order:
+                sums[p, 0, c].arrived()
+                sums[p, 1, c].arrived()
+                value = acc[p, cross_spot[p], pl.ds(256 * c, 256), :] + near_in[p, 0, c].astype(F32)
+                value = value + near_in[p, 1, c].astype(F32)
+                out[:, 256 * c:256 * c + 256] = value.T.astype(BF16)
 
     for p in range(2):
         for slot in range(3):
@@ -480,13 +496,13 @@
             pltpu.VMEM((2, width, rows), BF16),
             pltpu.VMEM((2, 3, width, rows), BF16),
             pltpu.VMEM((2, 3, 4, rows, 256), BF16),
-            pltpu.VMEM((2, 2, 512, 256), BF16),
-            pltpu.VMEM((2, 2, 512, 256), BF16),
-            pltpu.VMEM((2, 2, 2, 512, 256), BF16),
-            pltpu.VMEM((2, 2, 2, 512, 256), BF16),
+            pltpu.VMEM((2, 4, 256, 256), BF16),
+            pltpu.VMEM((2, 4, 256, 256), BF16),
+            pltpu.VMEM((2, 2, 4, 256, 256), BF16),
+            pltpu.VMEM((2, 2, 4, 256, 256), BF16),
             dma((3,)), dma((WSLOTS, 2)),
             *pair(4, docs), *pair(4, 7), *pair(2, 3), *pair(2, 8),
-            *pair(2, 4, 2), *pair(2, 4), *pair(2, 2), *pair(2, 4),
+            *pair(2, 8, 2), *pair(2, 8), *pair(2, 4), *pair(2, 8),
         ],
         compiler_params=pltpu.CompilerParams(collective_id=0, has_side_effects=True, vmem_limit_bytes=60 << 20),
         name="routed",

time: 102 us -> 98.8 us (0.969)
  Pallas kernels: 100 us -> 97.8 us
    pallas_call x1, Pallas kernels: 99.2 us -> 96.6 us  [shards(): pl.pallas_call(functools.partial(kernel, docs), out_shape=[pltpu.VMEM((co...]
where the time goes in v5:
time: 98.8 us; the launch traced here: 98.6 us
  Pallas kernels  97.8 us (99%)
    pallas_call x1, Pallas kernels, shards(): pl.pallas_call(functools.partial(kernel, docs), out_shape=[pltpu.VMEM((co...  96.6 us

profile of v5, /device:TPU:1, one launch (start us, length us, event | category | flops | bytes accessed | tf_op | source)
XLA Modules:
  0.0 98.6 jit_solution(9386647518004809877)
XLA Ops:
  0.6 96.6 %routed.1 = (bf16[256,1024]{1,0:T(8,128)(2,1)S(1)}, bf16[256,1024]{1,0:T(8,128)(2,1)S(1)}, bf16[256,1024]{1,0:T(8,128)(2,1)S(1)}) custom-call(s32[64,128]{1,0:T(8,128)} %bitcast.6, s32[64,128]{1,0:T(8,128)} %bitcast.7, s32[16]{0:T(128)} %len_ref.1, s32[16]{0:T(128)} %off_ref.1, bf16[256,1024]{1,0:T(8,128)(2,1)} %q_hbm.1, bf16[512,512]{1,0:T(8,128)(2,1)} %s_hbm.1, ...), custom_call_target="tpu_custom_call" | custom-call | tf_op jit(solution)/shard_map/routed/pallas_call | solution.py:481
  97.3 1.2 %hand_over.1 = (bf16[256,1024]{1,0:T(8,128)(2,1)}, bf16[256,1024]{1,0:T(8,128)(2,1)}, bf16[256,1024]{1,0:T(8,128)(2,1)}) custom-call(bf16[256,1024]{1,0:T(8,128)(2,1)S(1)} %get-tuple-element.6.refs_0_, bf16[256,1024]{1,0:T(8,128)(2,1)S(1)} %get-tuple-element.7.refs_1_, bf16[256,1024]{1,0:T(8,128)(2,1)S(1)} %get-tuple-element.8.refs_2_), custom_call_target="tpu_custom_call" | custom-call | tf_op jit(solution)/shard_map/hand_over/pallas_call | solution.py:511

commit v6 on v5

--- a/solution.py
+++ b/solution.py
@@ -394,9 +394,10 @@
     second_far(0)
     second_all(0)
     near_grads(0)
-    for k in (2, 1, -1):
-        near_block(0, k)
+    near_block(0, 2)
     second_far(1)
+    near_block(0, 1)
+    near_block(0, -1)
     second_all(1)
     near_grads(1)
     near_block(1, 2)

time: 98.8 us -> 98.8 us (level)
  no operation moved by 1% of the time
where the time goes in v6:
time: 98.8 us; the launch traced here: 98.6 us
  Pallas kernels  97.8 us (99%)
    pallas_call x1, Pallas kernels, shards(): pl.pallas_call(functools.partial(kernel, docs), out_shape=[pltpu.VMEM((co...  96.6 us

profile of v6, /device:TPU:1, one launch (start us, length us, event | category | flops | bytes accessed | tf_op | source)
XLA Modules:
  0.0 98.6 jit_solution(13914572176872407005)
XLA Ops:
  0.6 96.6 %routed.1 = (bf16[256,1024]{1,0:T(8,128)(2,1)S(1)}, bf16[256,1024]{1,0:T(8,128)(2,1)S(1)}, bf16[256,1024]{1,0:T(8,128)(2,1)S(1)}) custom-call(s32[64,128]{1,0:T(8,128)} %bitcast.6, s32[64,128]{1,0:T(8,128)} %bitcast.7, s32[16]{0:T(128)} %len_ref.1, s32[16]{0:T(128)} %off_ref.1, bf16[256,1024]{1,0:T(8,128)(2,1)} %q_hbm.1, bf16[512,512]{1,0:T(8,128)(2,1)} %s_hbm.1, ...), custom_call_target="tpu_custom_call" | custom-call | tf_op jit(solution)/shard_map/routed/pallas_call | solution.py:482
  97.3 1.2 %hand_over.1 = (bf16[256,1024]{1,0:T(8,128)(2,1)}, bf16[256,1024]{1,0:T(8,128)(2,1)}, bf16[256,1024]{1,0:T(8,128)(2,1)}) custom-call(bf16[256,1024]{1,0:T(8,128)(2,1)S(1)} %get-tuple-element.6.refs_0_, bf16[256,1024]{1,0:T(8,128)(2,1)S(1)} %get-tuple-element.7.refs_1_, bf16[256,1024]{1,0:T(8,128)(2,1)S(1)} %get-tuple-element.8.refs_2_), custom_call_target="tpu_custom_call" | custom-call | tf_op jit(solution)/shard_map/hand_over/pallas_call | solution.py:512
